TPU v7x, 256 devices: a whole 4x4x8 slice. The times are simulated.
256 devices in a mesh: ply: 4 (over z_hi, core), tile: 64 (over z_lo, y, x).
Axes of the slice: x: 4, y: 4, z: 8 (z_hi: 2, z_lo: 4; z = z_hi * 4 + z_lo), core: 2. Of those that a mesh axis runs over, the one named last changes fastest.
Arguments:
- displacement: float32 [3, 24, 512, 1024], P(None, 'ply', 'tile'), may hold values from -0.2 to 0.2
- angle_index: int32 [24], P('ply'), may hold values from 0 to 3
- bond_table: float32 [4, 14], replicated, may hold values from 5 to 50
- interface_stiffness: float32 [23], replicated, may hold values from 2 to 20
Outputs:
- force_density: float32 [3, 24, 512, 1024], P(None, 'ply', 'tile')
Inputs may be any that keep to these rules, and one draw needn't show every extreme that they name: `angle_index`: each ply's fibre orientation is an index into the rows of bond_table.
All inputs are finite; a program needn't handle non-finite values.
Results may differ from a plain program's by a relative error of at most 0.000058.
Values sent between devices are 32-bit elements; how exact they have to be, the bound alone decides.
A program may use at most 128 MiB of HBM per device.

v0:
```python
import math

import jax
import jax.numpy as jnp
from jax import lax
from jax.sharding import PartitionSpec as P

bulk_modulus = 40.0


def padded_2(shard, sides, width):
    for axis, dim in sides:
        peers, length = (lax.axis_size(axis), shard.shape[dim])
        up = [(i, (i + 1) % peers) for i in range(peers - 1)]
        down = [(j, i) for i, j in up]
        last = lax.slice_in_dim(shard, length - width, length, axis=dim)
        first = lax.slice_in_dim(shard, 0, width, axis=dim)
        before = lax.ppermute(last, axis, up)
        after = lax.ppermute(first, axis, down)
        shard = jnp.concatenate([before, shard, after], axis=dim)
    return shard


def bond_list():
    halves = []
    for shift_x in range(-3, 4):
        for shift_y in range(-3, 4):
            radius = shift_x * shift_x + shift_y * shift_y
            if 0 < radius <= 9 and (shift_x > 0 or (shift_x == 0 and shift_y > 0)):
                halves.append((shift_x, shift_y))
    result = []
    for shift_x in range(-3, 4):
        for shift_y in range(-3, 4):
            radius = shift_x * shift_x + shift_y * shift_y
            if 0 < radius <= 9:
                if (shift_x, shift_y) in halves:
                    column = halves.index((shift_x, shift_y))
                else:
                    column = halves.index((-shift_x, -shift_y))
                result.append((shift_x, shift_y, math.sqrt(radius), column))
    return result


def inside(x_coord, y_coord, shift_x, shift_y, x_total, y_total):
    x_next = x_coord + shift_x
    y_next = y_coord + shift_y
    return (x_next >= 0) & (x_next < x_total) & (y_next >= 0) & (y_next < y_total)


def weight_sum(x_coord, y_coord, x_total, y_total):
    total = jnp.zeros((x_coord.shape[0], y_coord.shape[1]), jnp.float32)
    for shift_x, shift_y, length, column in bond_list():
        total = total + jnp.where(
            inside(x_coord, y_coord, shift_x, shift_y, x_total, y_total), length, 0.0
        )
    return total


def stretch(anchor, neighbour, shift_x, shift_y, length):
    gap = neighbour - anchor
    sep_x = shift_x + gap[0]
    sep_y = shift_y + gap[1]
    sep_z = gap[2]
    span = jnp.sqrt(sep_x * sep_x + sep_y * sep_y + sep_z * sep_z)
    return (sep_x, sep_y, sep_z, span, span - length)


def bond_terms(theta_here, mass_here, theta_there, mass_there, shear, extension, length):
    first_side = 3.0 * bulk_modulus * theta_here / mass_here + 15.0 * shear * (
        extension - theta_here * length / 3.0
    ) / (mass_here * length)
    second_side = 3.0 * bulk_modulus * theta_there / mass_there + 15.0 * shear * (
        extension - theta_there * length / 3.0
    ) / (mass_there * length)
    return first_side + second_side


def local(displacement, angle_index, bond_table, interface_stiffness):
    comp_count, ply_count, col_count, row_count = displacement.shape
    x_total = col_count * lax.axis_size("tile")
    x_first = lax.axis_index("tile") * col_count
    bond_set = bond_list()
    y_grid = jnp.arange(row_count, dtype=jnp.int32)[None, :]
    y_wide = jnp.arange(-3, row_count + 3, dtype=jnp.int32)[None, :]
    padded = padded_2(displacement, (("tile", 2),), 3)
    margin = 0
    padded = jnp.pad(padded, ((0, 0), (0, 0), (0, 0), (3, 3)))
    border = margin + 3
    span_count = col_count + 2 * margin
    x_region = x_first - margin + jnp.arange(span_count, dtype=jnp.int32)[:, None]
    mass_region = weight_sum(x_region, y_grid, x_total, row_count)
    mass_region = jnp.where(mass_region > 0, mass_region, 1.0)
    anchor = padded[:, :, 3 : 3 + span_count, 3 : 3 + row_count]
    dilation = jnp.zeros((ply_count, span_count, row_count), jnp.float32)
    for shift_x, shift_y, length, column in bond_set:
        neighbour = padded[
            :, :, 3 + shift_x : 3 + shift_x + span_count, 3 + shift_y : 3 + shift_y + row_count
        ]
        stretched = stretch(anchor, neighbour, shift_x, shift_y, length)
        dilation = dilation + jnp.where(
            inside(x_region, y_grid, shift_x, shift_y, x_total, row_count), stretched[4], 0.0
        )
    dilation = 3.0 * dilation / mass_region
    theta_wide = padded_2(dilation, (("tile", 1),), 3)
    theta_wide = jnp.pad(theta_wide, ((0, 0), (0, 0), (3, 3)))
    x_wide = x_first - 3 + jnp.arange(col_count + 6, dtype=jnp.int32)[:, None]
    mass_wide = weight_sum(x_wide, y_wide, x_total, row_count)
    mass_wide = jnp.where(mass_wide > 0, mass_wide, 1.0)
    mass_here = mass_wide[3 : 3 + col_count, 3 : 3 + row_count]
    theta_here = theta_wide[:, 3 : 3 + col_count, 3 : 3 + row_count]
    x_core = x_first + jnp.arange(col_count, dtype=jnp.int32)[:, None]
    selector = (
        angle_index[:, None] == jnp.arange(bond_table.shape[0], dtype=jnp.int32)[None, :]
    ).astype(jnp.float32)
    shear_table = jnp.dot(selector, bond_table, precision=lax.Precision.HIGHEST)
    core = padded[:, :, border : border + col_count, 3 : 3 + row_count]
    force_x = jnp.zeros((ply_count, col_count, row_count), jnp.float32)
    force_y = jnp.zeros((ply_count, col_count, row_count), jnp.float32)
    force_z = jnp.zeros((ply_count, col_count, row_count), jnp.float32)
    for shift_x, shift_y, length, column in bond_set:
        neighbour = padded[
            :,
            :,
            border + shift_x : border + shift_x + col_count,
            3 + shift_y : 3 + shift_y + row_count,
        ]
        sep_x, sep_y, sep_z, span, extension = stretch(core, neighbour, shift_x, shift_y, length)
        theta_there = theta_wide[
            :, 3 + shift_x : 3 + shift_x + col_count, 3 + shift_y : 3 + shift_y + row_count
        ]
        mass_there = mass_wide[
            3 + shift_x : 3 + shift_x + col_count, 3 + shift_y : 3 + shift_y + row_count
        ]
        shear = shear_table[:, column][:, None, None]
        scalar = bond_terms(
            theta_here, mass_here, theta_there, mass_there, shear, extension, length
        )
        scalar = jnp.where(
            inside(x_core, y_grid, shift_x, shift_y, x_total, row_count), scalar / span, 0.0
        )
        force_x = force_x + scalar * sep_x
        force_y = force_y + scalar * sep_y
        force_z = force_z + scalar * sep_z
    zero_end = jnp.zeros((1,), jnp.float32)
    coupling = jnp.concatenate([zero_end, interface_stiffness, zero_end])
    local_coupling = lax.dynamic_slice_in_dim(
        coupling, lax.axis_index("ply") * ply_count, ply_count + 1
    )
    above = local_coupling[1:][None, :, None, None]
    below = local_coupling[:-1][None, :, None, None]
    stacked = padded_2(displacement, (("ply", 1),), 1)
    upper = stacked[:, 2:]
    lower = stacked[:, :-2]
    layered = above * (upper - displacement) + below * (lower - displacement)
    return jnp.stack([force_x, force_y, force_z]) + layered


def solution(mesh):
    placed = (P(None, "ply", "tile", None), P("ply"), P(), P())
    return jax.shard_map(
        local, mesh=mesh, in_specs=placed, out_specs=P(None, "ply", "tile", None), check_vma=False
    )
```

profile of v0, /device:TPU:31, one launch (start us, length us, event | category | flops | bytes accessed | tf_op | source)
XLA Modules:
  0.0 71.0 jit_solution(3223657829734447290)
XLA Ops:
  0.0 1.4 %fusion.116 = (f32[3,6,3,1024]{3,2,1,0:T(4,128)S(1)}, f32[3,6,3,1024]{3,2,1,0:T(4,128)S(1)}) fusion(f32[3,6,8,1024]{3,2,1,0:T(8,128)} %param.4), kind=kLoop, calls=%fused_computation.445 | loop fusion | bytes 884736 | tf_op jit(solution)/shard_map/slice | solution.py:16
  1.4 3.1 %collective-permute-start = (f32[3,6,3,1024]{3,2,1,0:T(4,128)S(1)}, f32[3,6,3,1024]{3,2,1,0:T(4,128)S(1)}, u32[]{:S(2)}, u32[]{:S(2)}) collective-permute-start(f32[3,6,3,1024]{3,2,1,0:T(4,128)S(1)} %get-tuple-element.84), channel_id=1, source_target_pairs={{0,1},{1,2},{2,3},{3,4},{4,5},{5,6},{6,7},{7,8},{8,9},{9,10},{10,1... | collective-permute-start | bytes 663560 | tf_op jit(solution)/shard_map/ppermute | solution.py:18
  4.5 2.2 %collective-permute-start.1 = (f32[3,6,3,1024]{3,2,1,0:T(4,128)S(1)}, f32[3,6,3,1024]{3,2,1,0:T(4,128)S(1)}, u32[]{:S(2)}, u32[]{:S(2)}) collective-permute-start(f32[3,6,3,1024]{3,2,1,0:T(4,128)S(1)} %get-tuple-element.85), channel_id=1, source_target_pairs={{1,0},{2,1},{3,2},{4,3},{5,4},{6,5},{7,6},{8,7},{9,8},{10,9},{11,1... | collective-permute-start | bytes 663560 | tf_op jit(solution)/shard_map/ppermute | solution.py:19
  6.7 1.6 %fusion.117 = (f32[3,1,8,1024]{3,2,1,0:T(8,128)}, f32[3,1,8,1024]{3,2,1,0:T(8,128)}) fusion(f32[3,6,8,1024]{3,2,1,0:T(8,128)} %param.4), kind=kLoop, calls=%fused_computation.446 | loop fusion | bytes 393216 | tf_op jit(solution)/shard_map/slice | solution.py:17
  8.3 3.1 %collective-permute-start.4 = (f32[3,1,8,1024]{3,2,1,0:T(8,128)}, f32[3,1,8,1024]{3,2,1,0:T(8,128)}, u32[]{:S(2)}, u32[]{:S(2)}) collective-permute-start(f32[3,1,8,1024]{3,2,1,0:T(8,128)} %get-tuple-element.86), channel_id=1, source_target_pairs={{64,0},{128,64},{192,128},{65,1},{129,65},{193,129},{66,2},{130,66... | collective-permute-start | bytes 294920 | tf_op jit(solution)/shard_map/ppermute | solution.py:19
  11.4 8.7 %collective-permute-start.5 = (f32[3,1,8,1024]{3,2,1,0:T(8,128)}, f32[3,1,8,1024]{3,2,1,0:T(8,128)}, u32[]{:S(2)}, u32[]{:S(2)}) collective-permute-start(f32[3,1,8,1024]{3,2,1,0:T(8,128)} %get-tuple-element.87), channel_id=1, source_target_pairs={{0,64},{64,128},{128,192},{1,65},{65,129},{129,193},{2,66},{66,130... | collective-permute-start | bytes 294920 | tf_op jit(solution)/shard_map/ppermute | solution.py:18
  20.3 0.9 %broadcast_and_fusion.5 = (pred[8,1024]{1,0:T(8,128)(4,1)S(1)}, pred[8,1024]{1,0:T(8,128)(4,1)}, pred[8,1024]{1,0:T(8,128)(4,1)}, pred[8,1024]{1,0:T(8,128)(4,1)...) fusion(pred[1024]{0:T(1024)(128)(4,1)S(1)} %iota_compare_fusion, ...), kind=kLoop, calls=%fused_computation.370 | loop fusion | flops 393216 | bytes 232504 | tf_op jit(solution)/shard_map/and | solution.py:47
  21.3 0.2 compare_select_fusion.1
  21.5 0.7 and_and_fusion.8
  22.3 0.4 compare_select_fusion
  22.7 0.2 fusion.119
  22.9 0.0 copy-start.44
  22.9 0.0 copy-start.45
  23.0 0.0 copy-start.1
  23.0 0.9 %broadcast_multiply_fusion.26 = (f32[8,1024]{1,0:T(8,128)S(1)}, f32[8,1024]{1,0:T(8,128)S(1)}, f32[8,1024]{1,0:T(8,128)S(1)}, f32[8,1024]{1,0:T(8,128)S(1)}, f32...) fusion(f32[14,1030]{1,0:T(8,128)S(1)} %compare_select_fusion), kind=kLoop, calls=%fused_computation.362 | loop fusion | flops 90112 | bytes 1015808 | tf_op jit(solution)/shard_map/mul | solution.py:74
  23.9 1.1 %fusion.120 = (f32[8,1024]{1,0:T(8,128)}, f32[8,1024]{1,0:T(8,128)}, f32[8,1024]{1,0:T(8,128)}, f32[8,1024]{1,0:T(8,128)}, f32[8,1024]{1,0:T(8,128)}, /*index=5*...) fusion(f32[14,1030]{1,0:T(8,128)S(1)} %compare_select_fusion), kind=kLoop, calls=%fused_computation.449 | loop fusion | bytes 1245184 | tf_op jit(solution)/shard_map/slice | solution.py:131
  25.0 0.7 slice.1042
  25.7 0.2 fusion.114
  25.9 0.1 pad_maximum_fusion.5
  25.9 0.1 dynamic_slice.3
  26.0 0.7 fusion.121
  26.7 0.0 collective-permute-done
  26.7 0.0 collective-permute-done.1
  26.7 0.8 %select_maximum_fusion = f32[3,6,14,1030]{3,2,1,0:T(8,128)S(1)} fusion(f32[3,6,3,1024]{3,2,1,0:T(4,128)S(1)} %collective-permute-done.1, f32[3,6,8,1024]{3,2,1,0:T(8,128)S(1)} %copy-done.1, f32[3,6,3,1024]{3,2,1,0:T(4,128)S(1)} %collective-permute-done), kind=kLoop, calls=%fused_computation.6 | loop fusion | flops 2076480 | bytes 2070432 | tf_op jit(solution)/shard_map/concatenate | solution.py:20
  27.5 2.8 %slice_subtract_fusion.1 = (f32[3,6,8,1024]{3,2,1,0:T(8,128)S(1)}, f32[3,6,8,1024]{3,2,1,0:T(8,128)S(1)}, f32[3,6,8,1024]{3,2,1,0:T(8,128)S(1)}, f32[3,6,8,1024]...) fusion(f32[3,6,8,1024]{3,2,1,0:T(8,128)S(1)} %copy-done.1, ...), kind=kLoop, calls=%fused_computation.24 | loop fusion | flops 2654207 | bytes 22413312 | tf_op jit(solution)/shard_map/sub | solution.py:60
  30.3 0.1 constant_dynamic-update-slice_fusion
  30.4 0.8 %slice_subtract_fusion = (f32[3,6,8,1024]{3,2,1,0:T(8,128)S(1)}, f32[3,6,8,1024]{3,2,1,0:T(8,128)S(1)}, f32[3,6,8,1024]{3,2,1,0:T(8,128)S(1)}, f32[3,6,8,1024]{3...) fusion(f32[3,6,8,1024]{3,2,1,0:T(8,128)S(1)} %copy-done.1, ...), kind=kLoop, calls=%fused_computation.23 | loop fusion | flops 1916928 | bytes 10838016 | tf_op jit(solution)/shard_map/sub | solution.py:60
  31.2 0.0 copy-done.34
  31.2 4.2 %fusion.63 = f32[6,8,1024]{2,1,0:T(8,128)S(1)} fusion(f32[8,1024]{1,0:T(8,128)S(1)} %compare_select_fusion.1, pred[8,1024]{1,0:T(8,128)(4,1)} %get-tuple-element.222, pred[8,1024]{1,0:T(8,128)(4,1)} %get-tuple-element.200, pred[8,1024]{1,0:T(8,128)(4,1)} %get-tuple-element.215, pred[8,1024]{1,0:T(8,128)(4,1)} %get-tuple-element.221, ...), kind=kLoop, calls=%fused_computation.203 | loop fusion | flops 13221888 | bytes 16973824 | tf_op jit(solution)/shard_map/div | solution.py:103
  35.9 6.6 %collective-permute-start.2 = (f32[6,3,1024]{2,1,0:T(4,128)S(1)}, f32[6,3,1024]{2,1,0:T(4,128)S(1)}, u32[]{:S(2)}, u32[]{:S(2)}) collective-permute-start(f32[6,3,1024]{2,1,0:T(4,128)S(1)} %get-tuple-element.89), channel_id=1, source_target_pairs={{0,1},{1,2},{2,3},{3,4},{4,5},{5,6},{6,7},{7,8},{8,9},{9,10},{10,1... | collective-permute-start | bytes 221192 | tf_op jit(solution)/shard_map/ppermute | solution.py:18
  42.5 1.9 %collective-permute-start.3 = (f32[6,3,1024]{2,1,0:T(4,128)S(1)}, f32[6,3,1024]{2,1,0:T(4,128)S(1)}, u32[]{:S(2)}, u32[]{:S(2)}) collective-permute-start(f32[6,3,1024]{2,1,0:T(4,128)S(1)} %get-tuple-element.88), channel_id=1, source_target_pairs={{1,0},{2,1},{3,2},{4,3},{5,4},{6,5},{7,6},{8,7},{9,8},{10,9},{11,1... | collective-permute-start | bytes 221192 | tf_op jit(solution)/shard_map/ppermute | solution.py:19
  44.4 0.4 multiply_reduce_fusion
  44.8 0.0 collective-permute-done.2
  44.8 7.2 %collective-permute-done.3 = f32[6,3,1024]{2,1,0:T(4,128)S(1)} collective-permute-done((f32[6,3,1024]{2,1,0:T(4,128)S(1)}, f32[6,3,1024]{2,1,0:T(4,128)S(1)}, u32[]{:S(2)}, u32[]{:S(2)}) %collective-permute-start.3) | collective-permute-done | bytes 73760 | tf_op jit(solution)/shard_map/ppermute | solution.py:19
  52.1 0.3 select_maximum_fusion.2
  52.4 0.0 copy-done.2
  52.4 0.0 copy-done.3
  52.4 0.0 copy-done.4
  52.4 0.0 copy-done.5
  52.4 0.0 copy-done.6
  52.4 0.0 copy-done.7
  52.4 0.0 copy-done.8
  52.4 0.0 copy-done.9
  52.4 0.0 copy-done.10
  52.4 0.0 copy-done.11
  52.5 0.0 copy-done.12
  52.5 0.0 copy-done.13
  52.5 0.0 copy-done.14
  52.5 0.0 copy-done.15
  52.5 0.0 copy-done.16
  52.5 0.0 copy-done.17
  52.5 0.0 copy-done.18
  52.5 0.0 copy-done.19
  52.5 0.0 copy-done.20
  52.5 0.0 copy-done.21
  52.6 0.0 copy-done.22
  52.6 0.0 copy-done.23
  52.6 0.0 copy-done.24
  52.7 13.6 %add_bitcast_fusion.2 = (f32[1,6,8,1024]{3,2,1,0:T(8,128)S(1)}, f32[6,8,1024]{2,1,0:T(8,128)S(1)}, f32[6,8,1024]{2,1,0:T(8,128)S(1)}, f32[6,8,1024]{2,1,0:T(8,12...) fusion(f32[3,6,8,1024]{3,2,1,0:T(8,128)S(1)} %get-tuple-element, ...), kind=kLoop, calls=%fused_computation.198 | loop fusion | flops 32833536 | bytes 29016400 | tf_op jit(solution)/shard_map/stack | solution.py:155
  66.4 1.3 %add_bitcast_fusion.1 = f32[1,6,8,1024]{3,2,1,0:T(8,128)S(1)} fusion(f32[6,8,1024]{2,1,0:T(8,128)S(1)} %get-tuple-element.47, f32[6,8,1024]{2,1,0:T(8,128)S(1)} %get-tuple-element.46, f32[6,8,1024]{2,1,0:T(8,128)S(1)} %get-tuple-element.45, f32[6,8,1024]{2,1,0:T(8,128)S(1)} %get-tuple-element.44, f32[6,8,1024]{2,1,0:T(8,128)S(1)} %get-tuple-element.43, ...), kind=kLoop, calls=%fused_computation.197 | loop fusion | flops 3784704 | bytes 11206656 | tf_op jit(solution)/shard_map/stack | solution.py:155
  67.7 1.3 %add_bitcast_fusion = f32[1,6,8,1024]{3,2,1,0:T(8,128)S(1)} fusion(f32[6,8,1024]{2,1,0:T(8,128)S(1)} %get-tuple-element.47, f32[6,8,1024]{2,1,0:T(8,128)S(1)} %get-tuple-element.46, f32[6,8,1024]{2,1,0:T(8,128)S(1)} %get-tuple-element.45, f32[6,8,1024]{2,1,0:T(8,128)S(1)} %get-tuple-element.44, f32[6,8,1024]{2,1,0:T(8,128)S(1)} %get-tuple-element.43, ...), kind=kLoop, calls=%fused_computation.196 | loop fusion | flops 2703360 | bytes 11206656 | tf_op jit(solution)/shard_map/stack | solution.py:155
  69.0 0.0 collective-permute-done.4
  69.0 0.0 collective-permute-done.5
  69.1 1.9 %fusion.8 = f32[3,6,8,1024]{3,2,1,0:T(8,128)} fusion(f32[3,6,8,1024]{3,2,1,0:T(8,128)S(1)} %copy-done.1, f32[3,1,8,1024]{3,2,1,0:T(8,128)} %collective-permute-done.5, f32[3,1,8,1024]{3,2,1,0:T(8,128)} %collective-permute-done.4, f32[1,6,8,1024]{3,2,1,0:T(8,128)S(1)} %add_bitcast_fusion, f32[1,6,8,1024]{3,2,1,0:T(8,128)S(1)} %add_bitcast_fusion.1, ...), kind=kLoop, calls=%fused_computation.19 | loop fusion | flops 1474560 | bytes 1966128 | tf_op jit(solution)/shard_map/add | solution.py:155
  (88 shorter events, 0.3 us)
Async XLA Ops:
  0.0 25.7 %copy-start = (f32[4,14]{1,0:T(4,128)S(1)}, f32[4,14]{1,0:T(4,128)}, u32[]{:S(2)}) copy-start(f32[4,14]{1,0:T(4,128)} %param.6) | copy-start | bytes 676
  1.4 25.3 %collective-permute-start = (f32[3,6,3,1024]{3,2,1,0:T(4,128)S(1)}, f32[3,6,3,1024]{3,2,1,0:T(4,128)S(1)}, u32[]{:S(2)}, u32[]{:S(2)}) collective-permute-start(f32[3,6,3,1024]{3,2,1,0:T(4,128)S(1)} %get-tuple-element.84), channel_id=1, source_target_pairs={{0,1},{1,2},{2,3},{3,4},{4,5},{5,6},{6,7},{7,8},{8,9},{9,10},{10,1... | collective-permute-start | bytes 663560 | tf_op jit(solution)/shard_map/ppermute | solution.py:18
  4.5 22.2 %collective-permute-start.1 = (f32[3,6,3,1024]{3,2,1,0:T(4,128)S(1)}, f32[3,6,3,1024]{3,2,1,0:T(4,128)S(1)}, u32[]{:S(2)}, u32[]{:S(2)}) collective-permute-start(f32[3,6,3,1024]{3,2,1,0:T(4,128)S(1)} %get-tuple-element.85), channel_id=1, source_target_pairs={{1,0},{2,1},{3,2},{4,3},{5,4},{6,5},{7,6},{8,7},{9,8},{10,9},{11,1... | collective-permute-start | bytes 663560 | tf_op jit(solution)/shard_map/ppermute | solution.py:19
  8.3 60.7 %collective-permute-start.4 = (f32[3,1,8,1024]{3,2,1,0:T(8,128)}, f32[3,1,8,1024]{3,2,1,0:T(8,128)}, u32[]{:S(2)}, u32[]{:S(2)}) collective-permute-start(f32[3,1,8,1024]{3,2,1,0:T(8,128)} %get-tuple-element.86), channel_id=1, source_target_pairs={{64,0},{128,64},{192,128},{65,1},{129,65},{193,129},{66,2},{130,66... | collective-permute-start | bytes 294920 | tf_op jit(solution)/shard_map/ppermute | solution.py:19
  11.4 57.6 %collective-permute-start.5 = (f32[3,1,8,1024]{3,2,1,0:T(8,128)}, f32[3,1,8,1024]{3,2,1,0:T(8,128)}, u32[]{:S(2)}, u32[]{:S(2)}) collective-permute-start(f32[3,1,8,1024]{3,2,1,0:T(8,128)} %get-tuple-element.87), channel_id=1, source_target_pairs={{0,64},{64,128},{128,192},{1,65},{65,129},{129,193},{2,66},{66,130... | collective-permute-start | bytes 294920 | tf_op jit(solution)/shard_map/ppermute | solution.py:18
  22.9 2.7 %copy-start.44 = (s32[6]{0:T(128)S(1)}, s32[6]{0:T(128)}, u32[]{:S(2)}) copy-start(s32[6]{0:T(128)} %param.5) | copy-start | bytes 76
  22.9 2.9 %copy-start.45 = (f32[23]{0:T(128)S(1)}, f32[23]{0:T(128)}, u32[]{:S(2)}) copy-start(f32[23]{0:T(128)} %param.7) | copy-start | bytes 280
  23.0 3.7 %copy-start.1 = (f32[3,6,8,1024]{3,2,1,0:T(8,128)S(1)}, f32[3,6,8,1024]{3,2,1,0:T(8,128)}, u32[]{:S(2)}) copy-start(f32[3,6,8,1024]{3,2,1,0:T(8,128)} %param.4) | copy-start | bytes 1769476
  30.4 0.9 %copy-start.34 = (pred[8,1024]{1,0:T(8,128)(4,1)S(1)}, pred[8,1024]{1,0:T(8,128)(4,1)}, u32[]{:S(2)}) copy-start(pred[8,1024]{1,0:T(8,128)(4,1)} %get-tuple-element.198) | copy-start | bytes 24580
  35.5 16.9 %copy-start.2 = (f32[8,1024]{1,0:T(8,128)S(1)}, f32[8,1024]{1,0:T(8,128)}, u32[]{:S(2)}) copy-start(f32[8,1024]{1,0:T(8,128)} %get-tuple-element.116) | copy-start | bytes 98308
  35.5 16.9 %copy-start.3 = (f32[8,1024]{1,0:T(8,128)S(1)}, f32[8,1024]{1,0:T(8,128)}, u32[]{:S(2)}) copy-start(f32[8,1024]{1,0:T(8,128)} %get-tuple-element.117) | copy-start | bytes 98308
  35.5 16.9 %copy-start.4 = (f32[8,1024]{1,0:T(8,128)S(1)}, f32[8,1024]{1,0:T(8,128)}, u32[]{:S(2)}) copy-start(f32[8,1024]{1,0:T(8,128)} %get-tuple-element.118) | copy-start | bytes 98308
  35.5 16.9 %copy-start.5 = (f32[8,1024]{1,0:T(8,128)S(1)}, f32[8,1024]{1,0:T(8,128)}, u32[]{:S(2)}) copy-start(f32[8,1024]{1,0:T(8,128)} %get-tuple-element.119) | copy-start | bytes 98308
  35.5 16.9 %copy-start.6 = (f32[8,1024]{1,0:T(8,128)S(1)}, f32[8,1024]{1,0:T(8,128)}, u32[]{:S(2)}) copy-start(f32[8,1024]{1,0:T(8,128)} %get-tuple-element.120) | copy-start | bytes 98308
  35.5 16.9 %copy-start.7 = (f32[8,1024]{1,0:T(8,128)S(1)}, f32[8,1024]{1,0:T(8,128)}, u32[]{:S(2)}) copy-start(f32[8,1024]{1,0:T(8,128)} %get-tuple-element.121) | copy-start | bytes 98308
  35.5 16.9 %copy-start.8 = (f32[8,1024]{1,0:T(8,128)S(1)}, f32[8,1024]{1,0:T(8,128)}, u32[]{:S(2)}) copy-start(f32[8,1024]{1,0:T(8,128)} %get-tuple-element.122) | copy-start | bytes 98308
  35.5 16.9 %copy-start.9 = (f32[8,1024]{1,0:T(8,128)S(1)}, f32[8,1024]{1,0:T(8,128)}, u32[]{:S(2)}) copy-start(f32[8,1024]{1,0:T(8,128)} %get-tuple-element.123) | copy-start | bytes 98308
  35.5 16.9 %copy-start.10 = (f32[8,1024]{1,0:T(8,128)S(1)}, f32[8,1024]{1,0:T(8,128)}, u32[]{:S(2)}) copy-start(f32[8,1024]{1,0:T(8,128)} %get-tuple-element.124) | copy-start | bytes 98308
  35.6 16.9 %copy-start.11 = (f32[8,1024]{1,0:T(8,128)S(1)}, f32[8,1024]{1,0:T(8,128)}, u32[]{:S(2)}) copy-start(f32[8,1024]{1,0:T(8,128)} %get-tuple-element.125) | copy-start | bytes 98308
  35.6 16.9 %copy-start.12 = (f32[8,1024]{1,0:T(8,128)S(1)}, f32[8,1024]{1,0:T(8,128)}, u32[]{:S(2)}) copy-start(f32[8,1024]{1,0:T(8,128)} %get-tuple-element.126) | copy-start | bytes 98308
  35.6 16.9 %copy-start.13 = (f32[8,1024]{1,0:T(8,128)S(1)}, f32[8,1024]{1,0:T(8,128)}, u32[]{:S(2)}) copy-start(f32[8,1024]{1,0:T(8,128)} %get-tuple-element.127) | copy-start | bytes 98308
  35.6 16.9 %copy-start.14 = (f32[8,1024]{1,0:T(8,128)S(1)}, f32[8,1024]{1,0:T(8,128)}, u32[]{:S(2)}) copy-start(f32[8,1024]{1,0:T(8,128)} %get-tuple-element.128) | copy-start | bytes 98308
  35.6 16.9 %copy-start.15 = (f32[8,1024]{1,0:T(8,128)S(1)}, f32[8,1024]{1,0:T(8,128)}, u32[]{:S(2)}) copy-start(f32[8,1024]{1,0:T(8,128)} %get-tuple-element.129) | copy-start | bytes 98308
  35.6 16.9 %copy-start.16 = (f32[8,1024]{1,0:T(8,128)S(1)}, f32[8,1024]{1,0:T(8,128)}, u32[]{:S(2)}) copy-start(f32[8,1024]{1,0:T(8,128)} %get-tuple-element.130) | copy-start | bytes 98308
  35.6 16.9 %copy-start.17 = (f32[8,1024]{1,0:T(8,128)S(1)}, f32[8,1024]{1,0:T(8,128)}, u32[]{:S(2)}) copy-start(f32[8,1024]{1,0:T(8,128)} %get-tuple-element.131) | copy-start | bytes 98308
  35.6 16.9 %copy-start.18 = (f32[8,1024]{1,0:T(8,128)S(1)}, f32[8,1024]{1,0:T(8,128)}, u32[]{:S(2)}) copy-start(f32[8,1024]{1,0:T(8,128)} %get-tuple-element.132) | copy-start | bytes 98308
  35.6 16.9 %copy-start.19 = (f32[8,1024]{1,0:T(8,128)S(1)}, f32[8,1024]{1,0:T(8,128)}, u32[]{:S(2)}) copy-start(f32[8,1024]{1,0:T(8,128)} %get-tuple-element.133) | copy-start | bytes 98308
  35.6 16.9 %copy-start.20 = (f32[8,1024]{1,0:T(8,128)S(1)}, f32[8,1024]{1,0:T(8,128)}, u32[]{:S(2)}) copy-start(f32[8,1024]{1,0:T(8,128)} %get-tuple-element.134) | copy-start | bytes 98308
  35.7 16.9 %copy-start.21 = (f32[8,1024]{1,0:T(8,128)S(1)}, f32[8,1024]{1,0:T(8,128)}, u32[]{:S(2)}) copy-start(f32[8,1024]{1,0:T(8,128)} %get-tuple-element.135) | copy-start | bytes 98308
  35.7 16.9 %copy-start.22 = (f32[8,1024]{1,0:T(8,128)S(1)}, f32[8,1024]{1,0:T(8,128)}, u32[]{:S(2)}) copy-start(f32[8,1024]{1,0:T(8,128)} %get-tuple-element.136) | copy-start | bytes 98308
  35.7 16.9 %copy-start.23 = (f32[8,1024]{1,0:T(8,128)S(1)}, f32[8,1024]{1,0:T(8,128)}, u32[]{:S(2)}) copy-start(f32[8,1024]{1,0:T(8,128)} %get-tuple-element.137) | copy-start | bytes 98308
  35.7 16.9 %copy-start.24 = (f32[8,1024]{1,0:T(8,128)S(1)}, f32[8,1024]{1,0:T(8,128)}, u32[]{:S(2)}) copy-start(f32[8,1024]{1,0:T(8,128)} %get-tuple-element.138) | copy-start | bytes 98308
  35.7 16.9 %copy-start.25 = (f32[8,1024]{1,0:T(8,128)S(1)}, f32[8,1024]{1,0:T(8,128)}, u32[]{:S(2)}) copy-start(f32[8,1024]{1,0:T(8,128)} %get-tuple-element.139) | copy-start | bytes 98308
  35.7 16.9 %copy-start.26 = (f32[8,1024]{1,0:T(8,128)S(1)}, f32[8,1024]{1,0:T(8,128)}, u32[]{:S(2)}) copy-start(f32[8,1024]{1,0:T(8,128)} %get-tuple-element.140) | copy-start | bytes 98308
  35.7 16.9 %copy-start.27 = (f32[8,1024]{1,0:T(8,128)S(1)}, f32[8,1024]{1,0:T(8,128)}, u32[]{:S(2)}) copy-start(f32[8,1024]{1,0:T(8,128)} %get-tuple-element.141) | copy-start | bytes 98308
  35.7 16.9 %copy-start.28 = (f32[8,1024]{1,0:T(8,128)S(1)}, f32[8,1024]{1,0:T(8,128)}, u32[]{:S(2)}) copy-start(f32[8,1024]{1,0:T(8,128)} %get-tuple-element.142) | copy-start | bytes 98308
  35.7 16.9 %copy-start.29 = (f32[8,1024]{1,0:T(8,128)S(1)}, f32[8,1024]{1,0:T(8,128)}, u32[]{:S(2)}) copy-start(f32[8,1024]{1,0:T(8,128)} %get-tuple-element.143) | copy-start | bytes 98308
  35.7 16.9 %copy-start.30 = (f32[8,1024]{1,0:T(8,128)S(1)}, f32[8,1024]{1,0:T(8,128)}, u32[]{:S(2)}) copy-start(f32[8,1024]{1,0:T(8,128)} %get-tuple-element.144) | copy-start | bytes 98308
  35.8 16.9 %copy-start.31 = (f32[8,1024]{1,0:T(8,128)S(1)}, f32[8,1024]{1,0:T(8,128)}, u32[]{:S(2)}) copy-start(f32[8,1024]{1,0:T(8,128)} %get-tuple-element.145) | copy-start | bytes 98308
  35.8 16.9 %copy-start.32 = (f32[8,1024]{1,0:T(8,128)S(1)}, f32[8,1024]{1,0:T(8,128)}, u32[]{:S(2)}) copy-start(f32[8,1024]{1,0:T(8,128)} %get-tuple-element.146) | copy-start | bytes 98308
  35.8 16.9 %copy-start.33 = (f32[8,1024]{1,0:T(8,128)S(1)}, f32[8,1024]{1,0:T(8,128)}, u32[]{:S(2)}) copy-start(f32[8,1024]{1,0:T(8,128)} %slice.1042) | copy-start | bytes 98308
  35.8 16.9 %copy-start.35 = (pred[8,1024]{1,0:T(8,128)(4,1)S(1)}, pred[8,1024]{1,0:T(8,128)(4,1)}, u32[]{:S(2)}) copy-start(pred[8,1024]{1,0:T(8,128)(4,1)} %get-tuple-element.199) | copy-start | bytes 24580
  35.8 16.9 %copy-start.36 = (pred[8,1024]{1,0:T(8,128)(4,1)S(1)}, pred[8,1024]{1,0:T(8,128)(4,1)}, u32[]{:S(2)}) copy-start(pred[8,1024]{1,0:T(8,128)(4,1)} %get-tuple-element.200) | copy-start | bytes 24580
  35.8 16.9 %copy-start.37 = (pred[8,1024]{1,0:T(8,128)(4,1)S(1)}, pred[8,1024]{1,0:T(8,128)(4,1)}, u32[]{:S(2)}) copy-start(pred[8,1024]{1,0:T(8,128)(4,1)} %get-tuple-element.201) | copy-start | bytes 24580
  35.8 16.9 %copy-start.38 = (pred[8,1024]{1,0:T(8,128)(4,1)S(1)}, pred[8,1024]{1,0:T(8,128)(4,1)}, u32[]{:S(2)}) copy-start(pred[8,1024]{1,0:T(8,128)(4,1)} %get-tuple-element.202) | copy-start | bytes 24580
  35.8 16.9 %copy-start.39 = (pred[8,1024]{1,0:T(8,128)(4,1)S(1)}, pred[8,1024]{1,0:T(8,128)(4,1)}, u32[]{:S(2)}) copy-start(pred[8,1024]{1,0:T(8,128)(4,1)} %get-tuple-element.203) | copy-start | bytes 24580
  35.8 16.9 %copy-start.40 = (pred[8,1024]{1,0:T(8,128)(4,1)S(1)}, pred[8,1024]{1,0:T(8,128)(4,1)}, u32[]{:S(2)}) copy-start(pred[8,1024]{1,0:T(8,128)(4,1)} %get-tuple-element.204) | copy-start | bytes 24580
  35.8 16.9 %copy-start.41 = (pred[8,1024]{1,0:T(8,128)(4,1)S(1)}, pred[8,1024]{1,0:T(8,128)(4,1)}, u32[]{:S(2)}) copy-start(pred[8,1024]{1,0:T(8,128)(4,1)} %get-tuple-element.205) | copy-start | bytes 24580
  35.9 8.9 %collective-permute-start.2 = (f32[6,3,1024]{2,1,0:T(4,128)S(1)}, f32[6,3,1024]{2,1,0:T(4,128)S(1)}, u32[]{:S(2)}, u32[]{:S(2)}) collective-permute-start(f32[6,3,1024]{2,1,0:T(4,128)S(1)} %get-tuple-element.89), channel_id=1, source_target_pairs={{0,1},{1,2},{2,3},{3,4},{4,5},{5,6},{6,7},{7,8},{8,9},{9,10},{10,1... | collective-permute-start | bytes 221192 | tf_op jit(solution)/shard_map/ppermute | solution.py:18
  42.5 9.6 %collective-permute-start.3 = (f32[6,3,1024]{2,1,0:T(4,128)S(1)}, f32[6,3,1024]{2,1,0:T(4,128)S(1)}, u32[]{:S(2)}, u32[]{:S(2)}) collective-permute-start(f32[6,3,1024]{2,1,0:T(4,128)S(1)} %get-tuple-element.88), channel_id=1, source_target_pairs={{1,0},{2,1},{3,2},{4,3},{5,4},{6,5},{7,6},{8,7},{9,8},{10,9},{11,1... | collective-permute-start | bytes 221192 | tf_op jit(solution)/shard_map/ppermute | solution.py:19
  67.7 1.3 %copy-start.42 = (f32[6]{0:T(128)S(1)}, f32[6]{0:T(128)}, u32[]{:S(2)}) copy-start(f32[6]{0:T(128)} %get-tuple-element.224) | copy-start | bytes 76
  67.7 1.3 %copy-start.43 = (f32[6]{0:T(128)S(1)}, f32[6]{0:T(128)}, u32[]{:S(2)}) copy-start(f32[6]{0:T(128)} %get-tuple-element.225) | copy-start | bytes 76
where the time goes:
time: 71.4 us; the launch traced here: 71 us
  other arithmetic  31.1 us (44%)
  starting transfers between devices  25.6 us (36%)
  waiting for transfers between devices  7.26 us (10%)
  local copies, waits for them, and re-layouts  5.82 us (8%)
  between operations  0.99 us (1%)
    ppermute x3, starting transfers between devices, padded_2(): before = lax.ppermute(last, axis, up)  18.4 us
    another operation x3, other arithmetic, local(): return jnp.stack([force_x, force_y, force_z]) + layered  16.2 us
    ppermute x3, waiting for transfers between devices, padded_2(): after = lax.ppermute(first, axis, down)  7.25 us
    ppermute x3, starting transfers between devices, padded_2(): after = lax.ppermute(first, axis, down)  7.22 us
    div x1, other arithmetic, local(): dilation = 3.0 * dilation / mass_region  4.22 us
    sub x2, other arithmetic, stretch(): gap = neighbour - anchor  3.62 us
    add x1, other arithmetic, local(): return jnp.stack([force_x, force_y, force_z]) + layered  1.95 us
    and x10, other arithmetic, inside(): (x_next >= 0) & (x_next < x_total) & (y_next >= 0) & (y_next < y_total)  1.65 us
  transfers between devices with their start and end apart: 6, of which 1 were waited for; matrix products, arithmetic and copies ran while one was open for 47% of the time, Pallas kernels for 0%

commit v1 on v0

v1 whole, which is shorter than its diff:
```python
import math

import jax
import jax.numpy as jnp
from jax import lax
from jax.experimental import pallas as pl
from jax.experimental.pallas import tpu as pltpu
from jax.sharding import PartitionSpec as P

bulk_modulus = 40.0


def bond_list():
    halves = []
    for shift_x in range(-3, 4):
        for shift_y in range(-3, 4):
            radius = shift_x * shift_x + shift_y * shift_y
            if 0 < radius <= 9 and (shift_x > 0 or (shift_x == 0 and shift_y > 0)):
                halves.append((shift_x, shift_y))
    result = []
    for shift_x in range(-3, 4):
        for shift_y in range(-3, 4):
            radius = shift_x * shift_x + shift_y * shift_y
            if 0 < radius <= 9:
                if (shift_x, shift_y) in halves:
                    column = halves.index((shift_x, shift_y))
                else:
                    column = halves.index((-shift_x, -shift_y))
                result.append((shift_x, shift_y, math.sqrt(radius), column))
    return result


def halo(shard, axis, dim, width):
    peers, length = lax.axis_size(axis), shard.shape[dim]
    up = [(i, (i + 1) % peers) for i in range(peers)]
    down = [(j, i) for i, j in up]
    last = lax.slice_in_dim(shard, length - width, length, axis=dim)
    first = lax.slice_in_dim(shard, 0, width, axis=dim)
    before = lax.ppermute(last, axis, up)
    after = lax.ppermute(first, axis, down)
    return jnp.concatenate([before, shard, after], axis=dim)


def shift_lanes(x, b):
    if b == 0:
        return x
    return pltpu.roll(x, (-b) % x.shape[-1], 1)


def make_kernel(cols, rows, x_total, nbond):
    bonds = bond_list()
    wide = cols + 6
    shifts = sorted({a for a, _, _, _ in bonds})
    lanes = sorted({b for _, b, _, _ in bonds})

    def kernel(x0_ref, coef_ref, u_ref, lo_ref, hi_ref, o_ref, wq_ref):
        p = pl.program_id(0)
        x0 = x0_ref[0]

        def masks(n, start):
            r = lax.broadcasted_iota(jnp.int32, (n, rows), 0) + (x0 + start)
            c = lax.broadcasted_iota(jnp.int32, (n, rows), 1)
            own = (r >= 0) & (r < x_total)
            xm = {a: own & (r + a >= 0) & (r + a < x_total) for a in shifts}
            ym = {b: (c + b >= 0) & (c + b < rows) for b in lanes}
            return xm, ym

        xm, ym = masks(wide, -3)
        mass = jnp.zeros((wide, rows), jnp.float32)
        for a, b, length, column in bonds:
            mass = mass + jnp.where(xm[a] & ym[b], length, 0.0)
        w = jnp.where(mass > 0, 1.0 / jnp.where(mass > 0, mass, 1.0), 0.0)
        ud = [u_ref[k, 0, 3:3 + wide, :] for k in range(3)]
        dil = jnp.zeros((wide, rows), jnp.float32)
        for a, b, length, column in bonds:
            nb = [shift_lanes(u_ref[k, 0, 3 + a:3 + a + wide, :], b) for k in range(3)]
            sx = (nb[0] - ud[0]) + a
            sy = (nb[1] - ud[1]) + b
            sz = nb[2] - ud[2]
            span = jnp.sqrt(sx * sx + sy * sy + sz * sz)
            dil = dil + jnp.where(xm[a] & ym[b], span - length, 0.0)
        theta = 3.0 * dil * w
        wq_ref[0] = w
        wq_ref[1] = theta * w

        xm, ym = masks(cols, 0)
        uc = [u_ref[k, 0, 6:6 + cols, :] for k in range(3)]
        wi = wq_ref[0, 3:3 + cols, :]
        qi = wq_ref[1, 3:3 + cols, :]
        fx = jnp.zeros((cols, rows), jnp.float32)
        fy = jnp.zeros((cols, rows), jnp.float32)
        fz = jnp.zeros((cols, rows), jnp.float32)
        for a, b, length, column in bonds:
            nb = [shift_lanes(u_ref[k, 0, 6 + a:6 + a + cols, :], b) for k in range(3)]
            wj = shift_lanes(wq_ref[0, 3 + a:3 + a + cols, :], b)
            qj = shift_lanes(wq_ref[1, 3 + a:3 + a + cols, :], b)
            sx = (nb[0] - uc[0]) + a
            sy = (nb[1] - uc[1]) + b
            sz = nb[2] - uc[2]
            span = jnp.sqrt(sx * sx + sy * sy + sz * sz)
            alpha = coef_ref[p, column]
            beta = coef_ref[p, nbond + column]
            t = alpha * (span - length) * (wi + wj) + beta * (qi + qj)
            f = jnp.where(xm[a] & ym[b], t / span, 0.0)
            fx = fx + f * sx
            fy = fy + f * sy
            fz = fz + f * sz
        above = coef_ref[p, 2 * nbond]
        below = coef_ref[p, 2 * nbond + 1]
        for k, fk in enumerate((fx, fy, fz)):
            hi = hi_ref[k, 0]
            lo = lo_ref[k, 0]
            o_ref[k, 0] = fk + (above * (hi - uc[k]) + below * (lo - uc[k]))

    return kernel


def local(displacement, angle_index, bond_table, interface_stiffness):
    comp_count, ply_count, col_count, row_count = displacement.shape
    nbond = bond_table.shape[1]
    x_total = col_count * lax.axis_size("tile")
    x0 = (lax.axis_index("tile") * col_count).astype(jnp.int32).reshape(1)
    lengths = [0.0] * nbond
    for a, b, length, column in bond_list():
        lengths[column] = length
    lengths = jnp.asarray(lengths, jnp.float32)
    selector = (
        angle_index[:, None] == jnp.arange(bond_table.shape[0], dtype=jnp.int32)[None, :]
    ).astype(jnp.float32)
    shear = jnp.dot(selector, bond_table, precision=lax.Precision.HIGHEST)
    alpha = 15.0 * shear / lengths[None, :]
    beta = 3.0 * bulk_modulus - 5.0 * shear
    zero_end = jnp.zeros((1,), jnp.float32)
    coupling = jnp.concatenate([zero_end, interface_stiffness, zero_end])
    local_coupling = lax.dynamic_slice_in_dim(
        coupling, lax.axis_index("ply") * ply_count, ply_count + 1
    )
    coef = jnp.concatenate(
        [alpha, beta, local_coupling[1:, None], local_coupling[:-1, None]], axis=1
    )
    ext = halo(displacement, "tile", 2, 6)
    stacked = halo(displacement, "ply", 1, 1)
    extended = col_count + 12
    kernel = make_kernel(col_count, row_count, x_total, nbond)
    smem = pltpu.MemorySpace.SMEM if hasattr(pltpu, "MemorySpace") else pltpu.SMEM
    return pl.pallas_call(
        kernel,
        grid=(ply_count,),
        in_specs=[
            pl.BlockSpec(memory_space=smem),
            pl.BlockSpec(memory_space=smem),
            pl.BlockSpec((3, 1, extended, row_count), lambda p: (0, p, 0, 0)),
            pl.BlockSpec((3, 1, col_count, row_count), lambda p: (0, p, 0, 0)),
            pl.BlockSpec((3, 1, col_count, row_count), lambda p: (0, p + 2, 0, 0)),
        ],
        out_specs=pl.BlockSpec((3, 1, col_count, row_count), lambda p: (0, p, 0, 0)),
        out_shape=jax.ShapeDtypeStruct(displacement.shape, jnp.float32),
        scratch_shapes=[pltpu.VMEM((2, col_count + 6, row_count), jnp.float32)],
    )(x0, coef, ext, stacked, stacked)


def solution(mesh):
    placed = (P(None, "ply", "tile", None), P("ply"), P(), P())
    return jax.shard_map(
        local, mesh=mesh, in_specs=placed, out_specs=P(None, "ply", "tile", None), check_vma=False
    )
```

time: 71.4 us -> 59.7 us (0.84)
  the two profiles are of different devices: /device:TPU:31 before, /device:TPU:1 now
where the time goes in v1:
time: 59.7 us; the launch traced here: 59.6 us
  Pallas kernels  22.6 us (38%)
  starting transfers between devices  16.5 us (28%)
  waiting for transfers between devices  15.3 us (26%)
  other arithmetic  3.21 us (5%)
  local copies, waits for them, and re-layouts  1.77 us (3%)
    pallas_call x1, Pallas kernels, local(): pl.pallas_call(kernel, grid=(ply_count,), in_specs=[pl.BlockSpec(memory_s...  22.6 us
    ppermute x2, starting transfers between devices, halo(): before = lax.ppermute(last, axis, up)  8.63 us
    ppermute x2, starting transfers between devices, halo(): after = lax.ppermute(first, axis, down)  7.87 us
    ppermute x2, waiting for transfers between devices, halo(): after = lax.ppermute(first, axis, down)  7.86 us
    ppermute x2, waiting for transfers between devices, halo(): before = lax.ppermute(last, axis, up)  7.47 us
    concatenate x2, other arithmetic, halo(): return jnp.concatenate([before, shard, after], axis=dim)  2.46 us
    slice x2, local copies, waits for them, and re-layouts, halo(): last = lax.slice_in_dim(shard, length - width, length, axis=dim)  1.41 us
  transfers between devices with their start and end apart: 4, of which 2 were waited for; matrix products, arithmetic and copies ran while one was open for 4% of the time, Pallas kernels for 0%

profile of v1, /device:TPU:1, one launch (start us, length us, event | category | flops | bytes accessed | tf_op | source)
XLA Modules:
  0.0 59.6 jit_solution(10299449246651054643)
XLA Ops:
  0.0 0.0 copy-start
  0.0 0.0 copy-start.4
  0.0 0.0 copy-start.1
  0.0 0.0 copy-start.2
  0.0 0.0 copy-start.3
  0.0 1.4 %fusion.3 = (f32[3,6,6,1024]{3,2,1,0:T(8,128)S(1)}, f32[3,6,6,1024]{3,2,1,0:T(8,128)S(1)}) fusion(f32[3,6,8,1024]{3,2,1,0:T(8,128)} %param.5), kind=kLoop, calls=%fused_computation.12 | loop fusion | bytes 1769472 | tf_op jit(solution)/shard_map/slice | solution.py:37
  1.4 2.1 %collective-permute-start = (f32[3,6,6,1024]{3,2,1,0:T(8,128)S(1)}, f32[3,6,6,1024]{3,2,1,0:T(8,128)S(1)}, u32[]{:S(2)}, u32[]{:S(2)}) collective-permute-start(f32[3,6,6,1024]{3,2,1,0:T(8,128)S(1)} %get-tuple-element.7), channel_id=1, source_target_pairs={{0,1},{1,2},{2,3},{3,4},{4,5},{5,6},{6,7},{7,8},{8,9},{9,10},{10,1... | collective-permute-start | bytes 1327112 | tf_op jit(solution)/shard_map/ppermute | solution.py:39
  3.5 7.9 %collective-permute-start.1 = (f32[3,6,6,1024]{3,2,1,0:T(8,128)S(1)}, f32[3,6,6,1024]{3,2,1,0:T(8,128)S(1)}, u32[]{:S(2)}, u32[]{:S(2)}) collective-permute-start(f32[3,6,6,1024]{3,2,1,0:T(8,128)S(1)} %get-tuple-element.8), channel_id=1, source_target_pairs={{1,0},{2,1},{3,2},{4,3},{5,4},{6,5},{7,6},{8,7},{9,8},{10,9},{11,1... | collective-permute-start | bytes 1327112 | tf_op jit(solution)/shard_map/ppermute | solution.py:40
  11.4 0.0 copy-done.1
  11.4 6.5 %collective-permute-start.2 = (f32[3,1,8,1024]{3,2,1,0:T(8,128)S(1)}, f32[3,1,8,1024]{3,2,1,0:T(8,128)S(1)}, u32[]{:S(2)}, u32[]{:S(2)}) collective-permute-start(f32[3,1,8,1024]{3,2,1,0:T(8,128)S(1)} %get-tuple-element.5), channel_id=1, source_target_pairs={{0,64},{64,128},{128,192},{192,0},{1,65},{65,129},{129,193},{193,1... | collective-permute-start | bytes 294920 | tf_op jit(solution)/shard_map/ppermute | solution.py:39
  17.9 0.0 collective-permute-start.3
  18.0 0.0 copy-done.2
  18.0 0.1 pad_maximum_fusion.3
  18.0 0.1 dynamic_slice.3
  18.1 0.1 slice_bitcast_fusion.1
  18.2 0.1 copy.6
  18.3 0.1 copy.7
  18.4 0.0 copy-done
  18.4 0.0 copy-done.4
  18.4 0.0 copy-done.3
  18.4 0.2 multiply_multiply_fusion
  18.6 0.7 %pad_maximum_fusion.2.coef_ref = f32[6,30]{1,0:T(8,128)} fusion(f32[6,1]{1,0:T(8,128)S(1)} %copy.7, f32[6,1]{1,0:T(8,128)S(1)} %copy.6, f32[6,14]{1,0:T(8,128)S(1)} %get-tuple-element.10, f32[6,14]{1,0:T(8,128)S(1)} %get-tuple-element.9), kind=kLoop, calls=%fused_computation.2 | loop fusion | flops 540 | bytes 1440 | tf_op jit(solution)/shard_map/concatenate | solution.py:138
  19.2 7.5 %collective-permute-done.2 = f32[3,1,8,1024]{3,2,1,0:T(8,128)S(1)} collective-permute-done((f32[3,1,8,1024]{3,2,1,0:T(8,128)S(1)}, f32[3,1,8,1024]{3,2,1,0:T(8,128)S(1)}, u32[]{:S(2)}, u32[]{:S(2)}) %collective-permute-start.2) | collective-permute-done | bytes 98336 | tf_op jit(solution)/shard_map/ppermute | solution.py:39
  26.7 7.9 %collective-permute-done.3 = f32[3,1,8,1024]{3,2,1,0:T(8,128)S(1)} collective-permute-done((f32[3,1,8,1024]{3,2,1,0:T(8,128)S(1)}, f32[3,1,8,1024]{3,2,1,0:T(8,128)S(1)}, u32[]{:S(2)}, u32[]{:S(2)}) %collective-permute-start.3) | collective-permute-done | bytes 98336 | tf_op jit(solution)/shard_map/ppermute | solution.py:40
  34.6 0.9 %pad_maximum_fusion.1.lo_ref.hi_ref = f32[3,8,8,1024]{3,2,1,0:T(8,128)} fusion(f32[3,1,8,1024]{3,2,1,0:T(8,128)S(1)} %collective-permute-done.3, f32[3,6,8,1024]{3,2,1,0:T(8,128)S(1)} %copy-done.1, f32[3,1,8,1024]{3,2,1,0:T(8,128)S(1)} %collective-permute-done.2), kind=kLoop, calls=%fused_computation.1 | loop fusion | flops 393216 | bytes 1572864 | tf_op jit(solution)/shard_map/concatenate | solution.py:41
  35.5 0.0 collective-permute-done
  35.5 0.0 collective-permute-done.1
  35.5 1.5 %pad_maximum_fusion.u_ref = f32[3,6,20,1024]{3,2,1,0:T(8,128)} fusion(f32[3,6,6,1024]{3,2,1,0:T(8,128)S(1)} %collective-permute-done.1, f32[3,6,8,1024]{3,2,1,0:T(8,128)S(1)} %copy-done.1, f32[3,6,6,1024]{3,2,1,0:T(8,128)S(1)} %collective-permute-done), kind=kLoop, calls=%fused_computation | loop fusion | flops 737280 | bytes 2949120 | tf_op jit(solution)/shard_map/concatenate | solution.py:41
  37.0 22.6 %shard_map.55 = f32[3,6,8,1024]{3,2,1,0:T(8,128)} custom-call(s32[1]{0:T(128)} %bitcast.x0_ref, f32[6,30]{1,0:T(8,128)} %pad_maximum_fusion.2.coef_ref, f32[3,6,20,1024]{3,2,1,0:T(8,128)} %pad_maximum_fusion.u_ref, f32[3,8,8,1024]{3,2,1,0:T(8,128)} %pad_maximum_fusion.1.lo_ref.hi_ref, f32[3,8,8,1024]{3,2,1,0:T(8,128)} %pad_maximum_fusion.1.lo_ref.hi_ref), custom_call_target="tpu_custom_call" | custom-call | tf_op jit(solution)/shard_map/pallas_call | solution.py:146
  (1 shorter events, 0.0 us)
Async XLA Ops:
  0.0 18.4 %copy-start = (f32[4,14]{1,0:T(4,128)S(1)}, f32[4,14]{1,0:T(4,128)}, u32[]{:S(2)}) copy-start(f32[4,14]{1,0:T(4,128)} %param.7) | copy-start | bytes 676
  0.0 18.4 %copy-start.4 = (f32[14]{0:T(128)S(1)}, f32[14]{0:T(128)}, u32[]{:S(2)}) copy-start(f32[14]{0:T(128)} %constant.30) | copy-start | bytes 172
  0.0 11.4 %copy-start.1 = (f32[3,6,8,1024]{3,2,1,0:T(8,128)S(1)}, f32[3,6,8,1024]{3,2,1,0:T(8,128)}, u32[]{:S(2)}) copy-start(f32[3,6,8,1024]{3,2,1,0:T(8,128)} %param.5) | copy-start | bytes 1769476
  0.0 17.9 %copy-start.2 = (f32[23]{0:T(128)S(1)}, f32[23]{0:T(128)}, u32[]{:S(2)}) copy-start(f32[23]{0:T(128)} %param.8) | copy-start | bytes 280
  0.0 18.4 %copy-start.3 = (s32[6]{0:T(128)S(1)}, s32[6]{0:T(128)}, u32[]{:S(2)}) copy-start(s32[6]{0:T(128)} %param.6) | copy-start | bytes 76
  1.4 34.1 %collective-permute-start = (f32[3,6,6,1024]{3,2,1,0:T(8,128)S(1)}, f32[3,6,6,1024]{3,2,1,0:T(8,128)S(1)}, u32[]{:S(2)}, u32[]{:S(2)}) collective-permute-start(f32[3,6,6,1024]{3,2,1,0:T(8,128)S(1)} %get-tuple-element.7), channel_id=1, source_target_pairs={{0,1},{1,2},{2,3},{3,4},{4,5},{5,6},{6,7},{7,8},{8,9},{9,10},{10,1... | collective-permute-start | bytes 1327112 | tf_op jit(solution)/shard_map/ppermute | solution.py:39
  3.5 32.0 %collective-permute-start.1 = (f32[3,6,6,1024]{3,2,1,0:T(8,128)S(1)}, f32[3,6,6,1024]{3,2,1,0:T(8,128)S(1)}, u32[]{:S(2)}, u32[]{:S(2)}) collective-permute-start(f32[3,6,6,1024]{3,2,1,0:T(8,128)S(1)} %get-tuple-element.8), channel_id=1, source_target_pairs={{1,0},{2,1},{3,2},{4,3},{5,4},{6,5},{7,6},{8,7},{9,8},{10,9},{11,1... | collective-permute-start | bytes 1327112 | tf_op jit(solution)/shard_map/ppermute | solution.py:40
  11.4 15.3 %collective-permute-start.2 = (f32[3,1,8,1024]{3,2,1,0:T(8,128)S(1)}, f32[3,1,8,1024]{3,2,1,0:T(8,128)S(1)}, u32[]{:S(2)}, u32[]{:S(2)}) collective-permute-start(f32[3,1,8,1024]{3,2,1,0:T(8,128)S(1)} %get-tuple-element.5), channel_id=1, source_target_pairs={{0,64},{64,128},{128,192},{192,0},{1,65},{65,129},{129,193},{193,1... | collective-permute-start | bytes 294920 | tf_op jit(solution)/shard_map/ppermute | solution.py:39
  17.9 16.6 %collective-permute-start.3 = (f32[3,1,8,1024]{3,2,1,0:T(8,128)S(1)}, f32[3,1,8,1024]{3,2,1,0:T(8,128)S(1)}, u32[]{:S(2)}, u32[]{:S(2)}) collective-permute-start(f32[3,1,8,1024]{3,2,1,0:T(8,128)S(1)} %get-tuple-element.6), channel_id=1, source_target_pairs={{64,0},{128,64},{192,128},{0,192},{65,1},{129,65},{193,129},{1,193... | collective-permute-start | bytes 294920 | tf_op jit(solution)/shard_map/ppermute | solution.py:40

commit v2 on v1

v2 whole, which is shorter than its diff:
```python
import math

import jax
import jax.numpy as jnp
from jax import lax
from jax.experimental import pallas as pl
from jax.experimental.pallas import tpu as pltpu
from jax.sharding import PartitionSpec as P

bulk_modulus = 40.0


def bond_list():
    halves = []
    for shift_x in range(-3, 4):
        for shift_y in range(-3, 4):
            radius = shift_x * shift_x + shift_y * shift_y
            if 0 < radius <= 9 and (shift_x > 0 or (shift_x == 0 and shift_y > 0)):
                halves.append((shift_x, shift_y))
    result = []
    for shift_x in range(-3, 4):
        for shift_y in range(-3, 4):
            radius = shift_x * shift_x + shift_y * shift_y
            if 0 < radius <= 9:
                if (shift_x, shift_y) in halves:
                    column = halves.index((shift_x, shift_y))
                else:
                    column = halves.index((-shift_x, -shift_y))
                result.append((shift_x, shift_y, math.sqrt(radius), column))
    return result


def halo(shard, axis, dim, width):
    peers, length = lax.axis_size(axis), shard.shape[dim]
    up = [(i, (i + 1) % peers) for i in range(peers)]
    down = [(j, i) for i, j in up]
    last = lax.slice_in_dim(shard, length - width, length, axis=dim)
    first = lax.slice_in_dim(shard, 0, width, axis=dim)
    before = lax.ppermute(last, axis, up)
    after = lax.ppermute(first, axis, down)
    return jnp.concatenate([before, shard, after], axis=dim)


def shift_lanes(x, b):
    if b == 0:
        return x
    return pltpu.roll(x, (-b) % x.shape[-1], 1)


MESH = pl.DeviceIdType.MESH


def make_kernel(plies, cols, rows, x_total, nbond):
    bonds = bond_list()
    wide = cols + 6
    shifts = sorted({a for a, _, _, _ in bonds})
    lanes = sorted({b for _, b, _, _ in bonds})

    def kernel(coef_ref, u_hbm, o_ref, ext, ply_halo, wq_ref, sems):
        t = lax.axis_index("tile")
        nt = lax.axis_size("tile")
        q = lax.axis_index("ply")
        nq = lax.axis_size("ply")
        x0 = t * cols
        own = pltpu.make_async_copy(u_hbm, ext.at[:, :, cols:2 * cols, :], sems.at[0])
        own.start()
        has = ((t > 0), (t < nt - 1), (q > 0), (q < nq - 1))
        peers = ({"tile": t - 1}, {"tile": t + 1}, {"ply": q - 1}, {"ply": q + 1})
        barrier = pltpu.get_barrier_semaphore()
        for cond, dev in zip(has, peers):
            @pl.when(cond)
            def _():
                pl.semaphore_signal(barrier, inc=1, device_id=dev, device_id_type=MESH)
        count = sum(c.astype(jnp.int32) for c in has)
        pl.semaphore_wait(barrier, count)
        copies = (
            pltpu.make_async_remote_copy(
                u_hbm, ext.at[:, :, 2 * cols:3 * cols, :], sems.at[1], sems.at[5],
                device_id=peers[0], device_id_type=MESH),
            pltpu.make_async_remote_copy(
                u_hbm, ext.at[:, :, 0:cols, :], sems.at[2], sems.at[6],
                device_id=peers[1], device_id_type=MESH),
            pltpu.make_async_remote_copy(
                u_hbm.at[:, 0], ply_halo.at[1], sems.at[3], sems.at[7],
                device_id=peers[2], device_id_type=MESH),
            pltpu.make_async_remote_copy(
                u_hbm.at[:, plies - 1], ply_halo.at[0], sems.at[4], sems.at[8],
                device_id=peers[3], device_id_type=MESH),
        )
        for cond, cp in zip(has, copies):
            pl.when(cond)(cp.start)

        r = lax.broadcasted_iota(jnp.int32, (wide, rows), 0) + (x0 - 3)
        c = lax.broadcasted_iota(jnp.int32, (wide, rows), 1)
        own_x = (r >= 0) & (r < x_total)
        mass = jnp.zeros((wide, rows), jnp.float32)
        for a, b, length, column in bonds:
            ok = own_x & (r + a >= 0) & (r + a < x_total) & (c + b >= 0) & (c + b < rows)
            mass = mass + jnp.where(ok, length, 0.0)
        wq_ref[0] = jnp.where(mass > 0, 1.0 / jnp.where(mass > 0, mass, 1.0), 0.0)

        @pl.when(t == 0)
        def _():
            ext[:, :, 0:cols, :] = jnp.zeros((3, plies, cols, rows), jnp.float32)

        @pl.when(t == nt - 1)
        def _():
            ext[:, :, 2 * cols:3 * cols, :] = jnp.zeros((3, plies, cols, rows), jnp.float32)

        @pl.when(q == 0)
        def _():
            ply_halo[0] = jnp.zeros((3, cols, rows), jnp.float32)

        @pl.when(q == nq - 1)
        def _():
            ply_halo[1] = jnp.zeros((3, cols, rows), jnp.float32)

        own.wait()
        pl.when(has[1])(copies[0].wait_recv)
        pl.when(has[0])(copies[1].wait_recv)
        pl.when(has[3])(copies[2].wait_recv)
        pl.when(has[2])(copies[3].wait_recv)

        def masks(n, start):
            r = lax.broadcasted_iota(jnp.int32, (n, rows), 0) + (x0 + start)
            c = lax.broadcasted_iota(jnp.int32, (n, rows), 1)
            own = (r >= 0) & (r < x_total)
            xm = {a: own & (r + a >= 0) & (r + a < x_total) for a in shifts}
            ym = {b: (c + b >= 0) & (c + b < rows) for b in lanes}
            return xm, ym

        base = cols - 3

        def ply_body(p, carry):
            xm, ym = masks(wide, -3)
            w = wq_ref[0]
            ud = [ext[k, p, base:base + wide, :] for k in range(3)]
            dil = jnp.zeros((wide, rows), jnp.float32)
            for a, b, length, column in bonds:
                nb = [shift_lanes(ext[k, p, base + a:base + a + wide, :], b) for k in range(3)]
                sx = (nb[0] - ud[0]) + a
                sy = (nb[1] - ud[1]) + b
                sz = nb[2] - ud[2]
                span = jnp.sqrt(sx * sx + sy * sy + sz * sz)
                dil = dil + jnp.where(xm[a] & ym[b], span - length, 0.0)
            theta = 3.0 * dil * w
            wq_ref[1] = theta * w

            xm, ym = masks(cols, 0)
            uc = [ext[k, p, cols:2 * cols, :] for k in range(3)]
            wi = wq_ref[0, 3:3 + cols, :]
            qi = wq_ref[1, 3:3 + cols, :]
            fx = jnp.zeros((cols, rows), jnp.float32)
            fy = jnp.zeros((cols, rows), jnp.float32)
            fz = jnp.zeros((cols, rows), jnp.float32)
            for a, b, length, column in bonds:
                nb = [shift_lanes(ext[k, p, cols + a:2 * cols + a, :], b) for k in range(3)]
                wj = shift_lanes(wq_ref[0, 3 + a:3 + a + cols, :], b)
                qj = shift_lanes(wq_ref[1, 3 + a:3 + a + cols, :], b)
                sx = (nb[0] - uc[0]) + a
                sy = (nb[1] - uc[1]) + b
                sz = nb[2] - uc[2]
                span = jnp.sqrt(sx * sx + sy * sy + sz * sz)
                alpha = coef_ref[p, column]
                beta = coef_ref[p, nbond + column]
                tb = alpha * (span - length) * (wi + wj) + beta * (qi + qj)
                f = jnp.where(xm[a] & ym[b], tb / span, 0.0)
                fx = fx + f * sx
                fy = fy + f * sy
                fz = fz + f * sz
            above = coef_ref[p, 2 * nbond]
            below = coef_ref[p, 2 * nbond + 1]
            hi_p = jnp.minimum(p + 1, plies - 1)
            lo_p = jnp.maximum(p - 1, 0)
            for k, fk in enumerate((fx, fy, fz)):
                hi = jnp.where(p == plies - 1, ply_halo[1, k], ext[k, hi_p, cols:2 * cols, :])
                lo = jnp.where(p == 0, ply_halo[0, k], ext[k, lo_p, cols:2 * cols, :])
                o_ref[k, p] = fk + (above * (hi - uc[k]) + below * (lo - uc[k]))
            return carry

        lax.fori_loop(0, plies, ply_body, 0)
        for cond, cp in zip(has, copies):
            pl.when(cond)(cp.wait_send)

    return kernel


def local(displacement, angle_index, bond_table, interface_stiffness):
    comp_count, ply_count, col_count, row_count = displacement.shape
    nbond = bond_table.shape[1]
    x_total = col_count * lax.axis_size("tile")
    lengths = [0.0] * nbond
    for a, b, length, column in bond_list():
        lengths[column] = length
    lengths = jnp.asarray(lengths, jnp.float32)
    selector = (
        angle_index[:, None] == jnp.arange(bond_table.shape[0], dtype=jnp.int32)[None, :]
    ).astype(jnp.float32)
    shear = jnp.dot(selector, bond_table, precision=lax.Precision.HIGHEST)
    alpha = 15.0 * shear / lengths[None, :]
    beta = 3.0 * bulk_modulus - 5.0 * shear
    zero_end = jnp.zeros((1,), jnp.float32)
    coupling = jnp.concatenate([zero_end, interface_stiffness, zero_end])
    local_coupling = lax.dynamic_slice_in_dim(
        coupling, lax.axis_index("ply") * ply_count, ply_count + 1
    )
    coef = jnp.concatenate(
        [alpha, beta, local_coupling[1:, None], local_coupling[:-1, None]], axis=1
    )
    kernel = make_kernel(ply_count, col_count, row_count, x_total, nbond)
    return pl.pallas_call(
        kernel,
        in_specs=[
            pl.BlockSpec(memory_space=pltpu.SMEM),
            pl.BlockSpec(memory_space=pl.ANY),
        ],
        out_specs=pl.BlockSpec(memory_space=pltpu.VMEM),
        out_shape=jax.ShapeDtypeStruct(displacement.shape, jnp.float32),
        scratch_shapes=[
            pltpu.VMEM((3, ply_count, 3 * col_count, row_count), jnp.float32),
            pltpu.VMEM((2, 3, col_count, row_count), jnp.float32),
            pltpu.VMEM((2, col_count + 6, row_count), jnp.float32),
            pltpu.SemaphoreType.DMA((9,)),
        ],
        compiler_params=pltpu.CompilerParams(collective_id=0, has_side_effects=True),
    )(coef, displacement)


def solution(mesh):
    placed = (P(None, "ply", "tile", None), P("ply"), P(), P())
    return jax.shard_map(
        local, mesh=mesh, in_specs=placed, out_specs=P(None, "ply", "tile", None), check_vma=False
    )
```

time: 59.7 us -> 54 us (0.905)
  the two profiles are of different devices: /device:TPU:1 before, /device:TPU:33 now
where the time goes in v2:
time: 54 us; the launch traced here: 53.8 us
  Pallas kernels  49.3 us (91%)
  local copies, waits for them, and re-layouts  3.52 us (7%)
  other arithmetic  0.76 us (1%)
    pallas_call x1, Pallas kernels, local(): pl.pallas_call(kernel, in_specs=[pl.BlockSpec(memory_space=pltpu.SMEM), p...  49.3 us
    unnamed x9, local copies, waits for them, and re-layouts  3.18 us

profile of v2, /device:TPU:33, one launch (start us, length us, event | category | flops | bytes accessed | tf_op | source)
XLA Modules:
  0.0 53.8 jit_solution(17779001935431144960)
XLA Ops:
  0.0 0.0 copy-start
  0.0 0.0 copy-start.1
  0.0 0.7 %copy-done.1 = f32[23]{0:T(128)S(1)} copy-done((f32[23]{0:T(128)S(1)}, f32[23]{0:T(128)}, u32[]{:S(2)}) %copy-start.1) | copy-done | bytes 116
  0.7 0.1 pad_maximum_fusion.1
  0.7 0.1 dynamic_slice.3
  0.8 0.1 slice_bitcast_fusion.1
  0.9 0.1 copy.6
  1.0 0.0 copy-start.2
  1.0 0.0 copy-start.3
  1.0 0.1 copy.7
  1.1 0.0 copy-done
  1.1 0.6 %copy-done.2 = s32[6]{0:T(128)S(1)} copy-done((s32[6]{0:T(128)S(1)}, s32[6]{0:T(128)}, u32[]{:S(2)}) %copy-start.2) | copy-done | bytes 48
  1.7 0.0 copy-done.3
  1.7 0.2 multiply_multiply_fusion
  1.9 0.7 %pad_maximum_fusion.coef_ref = f32[6,30]{1,0:T(8,128)} fusion(f32[6,1]{1,0:T(8,128)S(1)} %copy.7, f32[6,1]{1,0:T(8,128)S(1)} %copy.6, f32[6,14]{1,0:T(8,128)S(1)} %get-tuple-element.6, f32[6,14]{1,0:T(8,128)S(1)} %get-tuple-element.5), kind=kLoop, calls=%fused_computation | loop fusion | flops 540 | bytes 1440 | tf_op jit(solution)/shard_map/concatenate | solution.py:207
  2.5 49.3 %shard_map.55 = f32[3,6,8,1024]{3,2,1,0:T(8,128)} custom-call(f32[6,30]{1,0:T(8,128)} %pad_maximum_fusion.coef_ref, f32[3,6,8,1024]{3,2,1,0:T(8,128)} %u_hbm.1), custom_call_target="tpu_custom_call" | custom-call | tf_op jit(solution)/shard_map/pallas_call | solution.py:211
  51.8 1.9 %copy.9 = f32[3,6,8,1024]{3,2,1,0:T(8,128)} copy(f32[3,6,8,1024]{3,2,1,0:T(8,128)} %shard_map.55) | data formatting | bytes 1179648
Async XLA Ops:
  0.0 1.1 %copy-start = (f32[4,14]{1,0:T(4,128)S(1)}, f32[4,14]{1,0:T(4,128)}, u32[]{:S(2)}) copy-start(f32[4,14]{1,0:T(4,128)} %param.7) | copy-start | bytes 676
  0.0 0.7 %copy-start.1 = (f32[23]{0:T(128)S(1)}, f32[23]{0:T(128)}, u32[]{:S(2)}) copy-start(f32[23]{0:T(128)} %param.8) | copy-start | bytes 280
  1.0 0.7 %copy-start.2 = (s32[6]{0:T(128)S(1)}, s32[6]{0:T(128)}, u32[]{:S(2)}) copy-start(s32[6]{0:T(128)} %param.6) | copy-start | bytes 76
  1.0 0.7 %copy-start.3 = (f32[14]{0:T(128)S(1)}, f32[14]{0:T(128)}, u32[]{:S(2)}) copy-start(f32[14]{0:T(128)} %constant.25) | copy-start | bytes 172

commit v3 on v2

--- a/solution.py
+++ b/solution.py
@@ -56,7 +56,7 @@
     shifts = sorted({a for a, _, _, _ in bonds})
     lanes = sorted({b for _, b, _, _ in bonds})
 
-    def kernel(coef_ref, u_hbm, o_ref, ext, ply_halo, wq_ref, sems):
+    def kernel(coef_ref, u_hbm, o_ref, ext, ply_halo, wq_ref, sems, send_t, recv_t):
         t = lax.axis_index("tile")
         nt = lax.axis_size("tile")
         q = lax.axis_index("ply")
@@ -73,21 +73,25 @@
                 pl.semaphore_signal(barrier, inc=1, device_id=dev, device_id_type=MESH)
         count = sum(c.astype(jnp.int32) for c in has)
         pl.semaphore_wait(barrier, count)
-        copies = (
+        def tile_copy(d, p):
+            rows_at = slice(2 * cols, 3 * cols) if d == 0 else slice(0, cols)
+            return pltpu.make_async_remote_copy(
+                u_hbm.at[:, p], ext.at[:, p, rows_at, :], send_t.at[d, p], recv_t.at[d, p],
+                device_id=peers[d], device_id_type=MESH)
+
+        ply_copies = (
             pltpu.make_async_remote_copy(
-                u_hbm, ext.at[:, :, 2 * cols:3 * cols, :], sems.at[1], sems.at[5],
-                device_id=peers[0], device_id_type=MESH),
-            pltpu.make_async_remote_copy(
-                u_hbm, ext.at[:, :, 0:cols, :], sems.at[2], sems.at[6],
-                device_id=peers[1], device_id_type=MESH),
-            pltpu.make_async_remote_copy(
-                u_hbm.at[:, 0], ply_halo.at[1], sems.at[3], sems.at[7],
+                u_hbm.at[:, 0], ply_halo.at[1], sems.at[1], sems.at[3],
                 device_id=peers[2], device_id_type=MESH),
             pltpu.make_async_remote_copy(
-                u_hbm.at[:, plies - 1], ply_halo.at[0], sems.at[4], sems.at[8],
+                u_hbm.at[:, plies - 1], ply_halo.at[0], sems.at[2], sems.at[4],
                 device_id=peers[3], device_id_type=MESH),
         )
-        for cond, cp in zip(has, copies):
+        ahead = min(2, plies)
+        for p in range(ahead):
+            for d in range(2):
+                pl.when(has[d])(tile_copy(d, p).start)
+        for cond, cp in zip(has[2:], ply_copies):
             pl.when(cond)(cp.start)
 
         r = lax.broadcasted_iota(jnp.int32, (wide, rows), 0) + (x0 - 3)
@@ -116,10 +120,6 @@
             ply_halo[1] = jnp.zeros((3, cols, rows), jnp.float32)
 
         own.wait()
-        pl.when(has[1])(copies[0].wait_recv)
-        pl.when(has[0])(copies[1].wait_recv)
-        pl.when(has[3])(copies[2].wait_recv)
-        pl.when(has[2])(copies[3].wait_recv)
 
         def masks(n, start):
             r = lax.broadcasted_iota(jnp.int32, (n, rows), 0) + (x0 + start)
@@ -132,6 +132,11 @@
         base = cols - 3
 
         def ply_body(p, carry):
+            for d in range(2):
+                pl.when(has[d] & (p + ahead < plies))(
+                    lambda d=d: tile_copy(d, jnp.minimum(p + ahead, plies - 1)).start())
+            pl.when(has[1])(tile_copy(0, p).wait_recv)
+            pl.when(has[0])(tile_copy(1, p).wait_recv)
             xm, ym = masks(wide, -3)
             w = wq_ref[0]
             ud = [ext[k, p, base:base + wide, :] for k in range(3)]
@@ -173,13 +178,24 @@
             hi_p = jnp.minimum(p + 1, plies - 1)
             lo_p = jnp.maximum(p - 1, 0)
             for k, fk in enumerate((fx, fy, fz)):
-                hi = jnp.where(p == plies - 1, ply_halo[1, k], ext[k, hi_p, cols:2 * cols, :])
-                lo = jnp.where(p == 0, ply_halo[0, k], ext[k, lo_p, cols:2 * cols, :])
+                hi = jnp.where(p == plies - 1, uc[k], ext[k, hi_p, cols:2 * cols, :])
+                lo = jnp.where(p == 0, uc[k], ext[k, lo_p, cols:2 * cols, :])
                 o_ref[k, p] = fk + (above * (hi - uc[k]) + below * (lo - uc[k]))
             return carry
 
         lax.fori_loop(0, plies, ply_body, 0)
-        for cond, cp in zip(has, copies):
+        pl.when(has[3])(ply_copies[0].wait_recv)
+        pl.when(has[2])(ply_copies[1].wait_recv)
+        below = coef_ref[0, 2 * nbond + 1]
+        above = coef_ref[plies - 1, 2 * nbond]
+        for k in range(3):
+            o_ref[k, 0] = o_ref[k, 0] + below * (ply_halo[0, k] - ext[k, 0, cols:2 * cols, :])
+            o_ref[k, plies - 1] = o_ref[k, plies - 1] + above * (
+                ply_halo[1, k] - ext[k, plies - 1, cols:2 * cols, :])
+        for p in range(plies):
+            for d in range(2):
+                pl.when(has[d])(tile_copy(d, p).wait_send)
+        for cond, cp in zip(has[2:], ply_copies):
             pl.when(cond)(cp.wait_send)
 
     return kernel
@@ -220,7 +236,9 @@
             pltpu.VMEM((3, ply_count, 3 * col_count, row_count), jnp.float32),
             pltpu.VMEM((2, 3, col_count, row_count), jnp.float32),
             pltpu.VMEM((2, col_count + 6, row_count), jnp.float32),
-            pltpu.SemaphoreType.DMA((9,)),
+            pltpu.SemaphoreType.DMA((5,)),
+            pltpu.SemaphoreType.DMA((2, ply_count)),
+            pltpu.SemaphoreType.DMA((2, ply_count)),
         ],
         compiler_params=pltpu.CompilerParams(collective_id=0, has_side_effects=True),
     )(coef, displacement)

time: 54 us -> 42.3 us (0.78)
  Pallas kernels: 49.3 us -> 37.6 us
    pallas_call x1, Pallas kernels: 49.3 us -> 37.6 us  [local(): pl.pallas_call(kernel, in_specs=[pl.BlockSpec(memory_space=pltpu.SMEM), p...]
where the time goes in v3:
time: 42.3 us; the launch traced here: 42.1 us
  Pallas kernels  37.6 us (89%)
  local copies, waits for them, and re-layouts  3.52 us (8%)
  other arithmetic  0.76 us (2%)
    pallas_call x1, Pallas kernels, local(): pl.pallas_call(kernel, in_specs=[pl.BlockSpec(memory_space=pltpu.SMEM), p...  37.6 us
    unnamed x9, local copies, waits for them, and re-layouts  3.18 us

profile of v3, /device:TPU:33, one launch (start us, length us, event | category | flops | bytes accessed | tf_op | source)
XLA Modules:
  0.0 42.1 jit_solution(14889266018175223811)
XLA Ops:
  0.0 0.0 copy-start
  0.0 0.0 copy-start.1
  0.0 0.7 %copy-done.1 = f32[23]{0:T(128)S(1)} copy-done((f32[23]{0:T(128)S(1)}, f32[23]{0:T(128)}, u32[]{:S(2)}) %copy-start.1) | copy-done | bytes 116
  0.7 0.1 pad_maximum_fusion.1
  0.7 0.1 dynamic_slice.3
  0.8 0.1 slice_bitcast_fusion.1
  0.9 0.1 copy.6
  1.0 0.0 copy-start.2
  1.0 0.0 copy-start.3
  1.0 0.1 copy.7
  1.1 0.0 copy-done
  1.1 0.6 %copy-done.2 = s32[6]{0:T(128)S(1)} copy-done((s32[6]{0:T(128)S(1)}, s32[6]{0:T(128)}, u32[]{:S(2)}) %copy-start.2) | copy-done | bytes 48
  1.7 0.0 copy-done.3
  1.7 0.2 multiply_multiply_fusion
  1.9 0.7 %pad_maximum_fusion.coef_ref = f32[6,30]{1,0:T(8,128)} fusion(f32[6,1]{1,0:T(8,128)S(1)} %copy.7, f32[6,1]{1,0:T(8,128)S(1)} %copy.6, f32[6,14]{1,0:T(8,128)S(1)} %get-tuple-element.6, f32[6,14]{1,0:T(8,128)S(1)} %get-tuple-element.5), kind=kLoop, calls=%fused_computation | loop fusion | flops 540 | bytes 1440 | tf_op jit(solution)/shard_map/concatenate | solution.py:223
  2.5 37.6 %shard_map.55 = f32[3,6,8,1024]{3,2,1,0:T(8,128)} custom-call(f32[6,30]{1,0:T(8,128)} %pad_maximum_fusion.coef_ref, f32[3,6,8,1024]{3,2,1,0:T(8,128)} %u_hbm.1), custom_call_target="tpu_custom_call" | custom-call | tf_op jit(solution)/shard_map/pallas_call | solution.py:227
  40.1 1.9 %copy.9 = f32[3,6,8,1024]{3,2,1,0:T(8,128)} copy(f32[3,6,8,1024]{3,2,1,0:T(8,128)} %shard_map.55) | data formatting | bytes 1179648
Async XLA Ops:
  0.0 1.1 %copy-start = (f32[4,14]{1,0:T(4,128)S(1)}, f32[4,14]{1,0:T(4,128)}, u32[]{:S(2)}) copy-start(f32[4,14]{1,0:T(4,128)} %param.7) | copy-start | bytes 676
  0.0 0.7 %copy-start.1 = (f32[23]{0:T(128)S(1)}, f32[23]{0:T(128)}, u32[]{:S(2)}) copy-start(f32[23]{0:T(128)} %param.8) | copy-start | bytes 280
  1.0 0.7 %copy-start.2 = (s32[6]{0:T(128)S(1)}, s32[6]{0:T(128)}, u32[]{:S(2)}) copy-start(s32[6]{0:T(128)} %param.6) | copy-start | bytes 76
  1.0 0.7 %copy-start.3 = (f32[14]{0:T(128)S(1)}, f32[14]{0:T(128)}, u32[]{:S(2)}) copy-start(f32[14]{0:T(128)} %constant.25) | copy-start | bytes 172

commit v4 on v3

--- a/solution.py
+++ b/solution.py
@@ -50,13 +50,14 @@
 MESH = pl.DeviceIdType.MESH
 
 
-def make_kernel(plies, cols, rows, x_total, nbond):
+def make_kernel(plies, cols, rows, x_total, nsprings):
     bonds = bond_list()
     wide = cols + 6
     shifts = sorted({a for a, _, _, _ in bonds})
     lanes = sorted({b for _, b, _, _ in bonds})
 
-    def kernel(coef_ref, u_hbm, o_ref, ext, ply_halo, wq_ref, sems, send_t, recv_t):
+    def kernel(angle_ref, table_ref, spring_ref, u_hbm, o_ref, ext, ply_halo, wq_ref, dmask_ref,
+               fmask_ref, sems, send_t, recv_t):
         t = lax.axis_index("tile")
         nt = lax.axis_size("tile")
         q = lax.axis_index("ply")
@@ -94,13 +95,20 @@
         for cond, cp in zip(has[2:], ply_copies):
             pl.when(cond)(cp.start)
 
-        r = lax.broadcasted_iota(jnp.int32, (wide, rows), 0) + (x0 - 3)
-        c = lax.broadcasted_iota(jnp.int32, (wide, rows), 1)
-        own_x = (r >= 0) & (r < x_total)
-        mass = jnp.zeros((wide, rows), jnp.float32)
-        for a, b, length, column in bonds:
-            ok = own_x & (r + a >= 0) & (r + a < x_total) & (c + b >= 0) & (c + b < rows)
-            mass = mass + jnp.where(ok, length, 0.0)
+        def bond_masks(n, start, out_ref):
+            r = lax.broadcasted_iota(jnp.int32, (n, rows), 0) + (x0 + start)
+            c = lax.broadcasted_iota(jnp.int32, (n, rows), 1)
+            own_x = (r >= 0) & (r < x_total)
+            total = jnp.zeros((n, rows), jnp.float32)
+            for i, (a, b, length, column) in enumerate(bonds):
+                ok = own_x & (r + a >= 0) & (r + a < x_total) & (c + b >= 0) & (c + b < rows)
+                m = jnp.where(ok, 1.0, 0.0)
+                out_ref[i] = m
+                total = total + m * length
+            return total
+
+        mass = bond_masks(wide, -3, dmask_ref)
+        bond_masks(cols, 0, fmask_ref)
         wq_ref[0] = jnp.where(mass > 0, 1.0 / jnp.where(mass > 0, mass, 1.0), 0.0)
 
         @pl.when(t == 0)
@@ -131,50 +139,65 @@
 
         base = cols - 3
 
+        groups = {}
+        for i, (a, b, length, column) in enumerate(bonds):
+            groups.setdefault(a, []).append((i, b, length, column))
+
         def ply_body(p, carry):
             for d in range(2):
                 pl.when(has[d] & (p + ahead < plies))(
                     lambda d=d: tile_copy(d, jnp.minimum(p + ahead, plies - 1)).start())
             pl.when(has[1])(tile_copy(0, p).wait_recv)
             pl.when(has[0])(tile_copy(1, p).wait_recv)
-            xm, ym = masks(wide, -3)
+            gp = q * plies + p
+            kind = angle_ref[p]
             w = wq_ref[0]
             ud = [ext[k, p, base:base + wide, :] for k in range(3)]
+            ud_y = {b: ud[1] - b for b in lanes}
             dil = jnp.zeros((wide, rows), jnp.float32)
-            for a, b, length, column in bonds:
-                nb = [shift_lanes(ext[k, p, base + a:base + a + wide, :], b) for k in range(3)]
-                sx = (nb[0] - ud[0]) + a
-                sy = (nb[1] - ud[1]) + b
-                sz = nb[2] - ud[2]
-                span = jnp.sqrt(sx * sx + sy * sy + sz * sz)
-                dil = dil + jnp.where(xm[a] & ym[b], span - length, 0.0)
+            for a, members in groups.items():
+                slab = [ext[k, p, base + a:base + a + wide, :] for k in range(3)]
+                ud_x = ud[0] - a
+                for i, b, length, column in members:
+                    sx = shift_lanes(slab[0], b) - ud_x
+                    sy = shift_lanes(slab[1], b) - ud_y[b]
+                    sz = shift_lanes(slab[2], b) - ud[2]
+                    s2 = sx * sx + sy * sy + sz * sz
+                    span = s2 * lax.rsqrt(s2)
+                    dil = dil + (span - length) * dmask_ref[i]
             theta = 3.0 * dil * w
             wq_ref[1] = theta * w
 
-            xm, ym = masks(cols, 0)
             uc = [ext[k, p, cols:2 * cols, :] for k in range(3)]
+            uc_y = {b: uc[1] - b for b in lanes}
             wi = wq_ref[0, 3:3 + cols, :]
             qi = wq_ref[1, 3:3 + cols, :]
             fx = jnp.zeros((cols, rows), jnp.float32)
             fy = jnp.zeros((cols, rows), jnp.float32)
             fz = jnp.zeros((cols, rows), jnp.float32)
-            for a, b, length, column in bonds:
-                nb = [shift_lanes(ext[k, p, cols + a:2 * cols + a, :], b) for k in range(3)]
-                wj = shift_lanes(wq_ref[0, 3 + a:3 + a + cols, :], b)
-                qj = shift_lanes(wq_ref[1, 3 + a:3 + a + cols, :], b)
-                sx = (nb[0] - uc[0]) + a
-                sy = (nb[1] - uc[1]) + b
-                sz = nb[2] - uc[2]
-                span = jnp.sqrt(sx * sx + sy * sy + sz * sz)
-                alpha = coef_ref[p, column]
-                beta = coef_ref[p, nbond + column]
-                tb = alpha * (span - length) * (wi + wj) + beta * (qi + qj)
-                f = jnp.where(xm[a] & ym[b], tb / span, 0.0)
-                fx = fx + f * sx
-                fy = fy + f * sy
-                fz = fz + f * sz
-            above = coef_ref[p, 2 * nbond]
-            below = coef_ref[p, 2 * nbond + 1]
+            for a, members in groups.items():
+                slab = [ext[k, p, cols + a:2 * cols + a, :] for k in range(3)]
+                w_slab = wq_ref[0, 3 + a:3 + a + cols, :]
+                q_slab = wq_ref[1, 3 + a:3 + a + cols, :]
+                uc_x = uc[0] - a
+                for i, b, length, column in members:
+                    sx = shift_lanes(slab[0], b) - uc_x
+                    sy = shift_lanes(slab[1], b) - uc_y[b]
+                    sz = shift_lanes(slab[2], b) - uc[2]
+                    s2 = sx * sx + sy * sy + sz * sz
+                    inv = lax.rsqrt(s2)
+                    span = s2 * inv
+                    shear = table_ref[kind, column]
+                    alpha = shear * (15.0 / length)
+                    beta = 3.0 * bulk_modulus - 5.0 * shear
+                    tb = alpha * (span - length) * (wi + shift_lanes(w_slab, b)) + beta * (
+                        qi + shift_lanes(q_slab, b))
+                    f = (tb * inv) * fmask_ref[i]
+                    fx = fx + f * sx
+                    fy = fy + f * sy
+                    fz = fz + f * sz
+            above = jnp.where(gp < nsprings, spring_ref[jnp.minimum(gp, nsprings - 1)], 0.0)
+            below = jnp.where(gp > 0, spring_ref[jnp.maximum(gp - 1, 0)], 0.0)
             hi_p = jnp.minimum(p + 1, plies - 1)
             lo_p = jnp.maximum(p - 1, 0)
             for k, fk in enumerate((fx, fy, fz)):
@@ -186,8 +209,10 @@
         lax.fori_loop(0, plies, ply_body, 0)
         pl.when(has[3])(ply_copies[0].wait_recv)
         pl.when(has[2])(ply_copies[1].wait_recv)
-        below = coef_ref[0, 2 * nbond + 1]
-        above = coef_ref[plies - 1, 2 * nbond]
+        g0 = q * plies
+        below = jnp.where(g0 > 0, spring_ref[jnp.maximum(g0 - 1, 0)], 0.0)
+        gl = q * plies + plies - 1
+        above = jnp.where(gl < nsprings, spring_ref[jnp.minimum(gl, nsprings - 1)], 0.0)
         for k in range(3):
             o_ref[k, 0] = o_ref[k, 0] + below * (ply_halo[0, k] - ext[k, 0, cols:2 * cols, :])
             o_ref[k, plies - 1] = o_ref[k, plies - 1] + above * (
@@ -203,45 +228,27 @@
 
 def local(displacement, angle_index, bond_table, interface_stiffness):
     comp_count, ply_count, col_count, row_count = displacement.shape
-    nbond = bond_table.shape[1]
     x_total = col_count * lax.axis_size("tile")
-    lengths = [0.0] * nbond
-    for a, b, length, column in bond_list():
-        lengths[column] = length
-    lengths = jnp.asarray(lengths, jnp.float32)
-    selector = (
-        angle_index[:, None] == jnp.arange(bond_table.shape[0], dtype=jnp.int32)[None, :]
-    ).astype(jnp.float32)
-    shear = jnp.dot(selector, bond_table, precision=lax.Precision.HIGHEST)
-    alpha = 15.0 * shear / lengths[None, :]
-    beta = 3.0 * bulk_modulus - 5.0 * shear
-    zero_end = jnp.zeros((1,), jnp.float32)
-    coupling = jnp.concatenate([zero_end, interface_stiffness, zero_end])
-    local_coupling = lax.dynamic_slice_in_dim(
-        coupling, lax.axis_index("ply") * ply_count, ply_count + 1
-    )
-    coef = jnp.concatenate(
-        [alpha, beta, local_coupling[1:, None], local_coupling[:-1, None]], axis=1
-    )
-    kernel = make_kernel(ply_count, col_count, row_count, x_total, nbond)
+    kernel = make_kernel(ply_count, col_count, row_count, x_total, interface_stiffness.shape[0])
+    nbond = len(bond_list())
+    smem = pl.BlockSpec(memory_space=pltpu.SMEM)
     return pl.pallas_call(
         kernel,
-        in_specs=[
-            pl.BlockSpec(memory_space=pltpu.SMEM),
-            pl.BlockSpec(memory_space=pl.ANY),
-        ],
+        in_specs=[smem, smem, smem, pl.BlockSpec(memory_space=pl.ANY)],
         out_specs=pl.BlockSpec(memory_space=pltpu.VMEM),
         out_shape=jax.ShapeDtypeStruct(displacement.shape, jnp.float32),
         scratch_shapes=[
             pltpu.VMEM((3, ply_count, 3 * col_count, row_count), jnp.float32),
             pltpu.VMEM((2, 3, col_count, row_count), jnp.float32),
             pltpu.VMEM((2, col_count + 6, row_count), jnp.float32),
+            pltpu.VMEM((nbond, col_count + 6, row_count), jnp.float32),
+            pltpu.VMEM((nbond, col_count, row_count), jnp.float32),
             pltpu.SemaphoreType.DMA((5,)),
             pltpu.SemaphoreType.DMA((2, ply_count)),
             pltpu.SemaphoreType.DMA((2, ply_count)),
         ],
         compiler_params=pltpu.CompilerParams(collective_id=0, has_side_effects=True),
-    )(coef, displacement)
+    )(angle_index, bond_table, interface_stiffness, displacement)
 
 
 def solution(mesh):

time: 42.3 us -> 37.6 us (0.89)
  Pallas kernels: 37.6 us -> 35.5 us
  local copies, waits for them, and re-layouts: 3.52 us -> 1.93 us
  other arithmetic: 0.76 us -> 0 us
    pallas_call x1, Pallas kernels: 37.6 us -> 35.5 us  [local(): pl.pallas_call(kernel, in_specs=[smem, smem, smem, pl.BlockSpec(memory_sp...]
    unnamed x9 -> x1, local copies, waits for them, and re-layouts: 3.18 us -> 1.93 us
    concatenate x2 -> x0, other arithmetic: 0.76 us -> none  [the longest x1 0.68 us: local(): jnp.concatenate([alpha, beta, local_coupling[1:, None], local_coupling[:-...]
where the time goes in v4:
time: 37.6 us; the launch traced here: 37.4 us
  Pallas kernels  35.5 us (94%)
  local copies, waits for them, and re-layouts  1.93 us (5%)
    pallas_call x1, Pallas kernels, local(): pl.pallas_call(kernel, in_specs=[smem, smem, smem, pl.BlockSpec(memory_sp...  35.5 us
    unnamed x1, local copies, waits for them, and re-layouts  1.93 us

profile of v4, /device:TPU:33, one launch (start us, length us, event | category | flops | bytes accessed | tf_op | source)
XLA Modules:
  0.0 37.4 jit_solution(8249777270527252636)
XLA Ops:
  0.0 35.5 %shard_map.46 = f32[3,6,8,1024]{3,2,1,0:T(8,128)} custom-call(s32[6]{0:T(128)} %angle_ref.1, f32[4,14]{1,0:T(4,128)} %table_ref.1, f32[23]{0:T(128)} %spring_ref.1, f32[3,6,8,1024]{3,2,1,0:T(8,128)} %u_hbm.1), custom_call_target="tpu_custom_call" | custom-call | tf_op jit(solution)/shard_map/pallas_call | solution.py:235
  35.5 1.9 %copy.6 = f32[3,6,8,1024]{3,2,1,0:T(8,128)} copy(f32[3,6,8,1024]{3,2,1,0:T(8,128)} %shard_map.46) | data formatting | bytes 1179648

commit v5 on v4

--- a/solution.py
+++ b/solution.py
@@ -56,7 +56,7 @@
     shifts = sorted({a for a, _, _, _ in bonds})
     lanes = sorted({b for _, b, _, _ in bonds})
 
-    def kernel(angle_ref, table_ref, spring_ref, u_hbm, o_ref, ext, ply_halo, wq_ref, dmask_ref,
+    def kernel(angle_ref, table_ref, spring_ref, u_hbm, o_ref, edge_ref, ext, ply_halo, wq_ref, dmask_ref,
                fmask_ref, sems, send_t, recv_t):
         t = lax.axis_index("tile")
         nt = lax.axis_size("tile")
@@ -214,9 +214,8 @@
         gl = q * plies + plies - 1
         above = jnp.where(gl < nsprings, spring_ref[jnp.minimum(gl, nsprings - 1)], 0.0)
         for k in range(3):
-            o_ref[k, 0] = o_ref[k, 0] + below * (ply_halo[0, k] - ext[k, 0, cols:2 * cols, :])
-            o_ref[k, plies - 1] = o_ref[k, plies - 1] + above * (
-                ply_halo[1, k] - ext[k, plies - 1, cols:2 * cols, :])
+            edge_ref[0, k] = below * (ply_halo[0, k] - ext[k, 0, cols:2 * cols, :])
+            edge_ref[1, k] = above * (ply_halo[1, k] - ext[k, plies - 1, cols:2 * cols, :])
         for p in range(plies):
             for d in range(2):
                 pl.when(has[d])(tile_copy(d, p).wait_send)
@@ -224,6 +223,14 @@
             pl.when(cond)(cp.wait_send)
 
     return kernel
+
+
+def add_edges(force_ref, edge_ref, o_ref):
+    plies = force_ref.shape[1]
+    o_ref[...] = force_ref[...]
+    for k in range(3):
+        o_ref[k, 0] = force_ref[k, 0] + edge_ref[0, k]
+        o_ref[k, plies - 1] = force_ref[k, plies - 1] + edge_ref[1, k]
 
 
 def local(displacement, angle_index, bond_table, interface_stiffness):
@@ -232,11 +239,15 @@
     kernel = make_kernel(ply_count, col_count, row_count, x_total, interface_stiffness.shape[0])
     nbond = len(bond_list())
     smem = pl.BlockSpec(memory_space=pltpu.SMEM)
-    return pl.pallas_call(
+    vmem = pl.BlockSpec(memory_space=pltpu.VMEM)
+    force, edges = pl.pallas_call(
         kernel,
         in_specs=[smem, smem, smem, pl.BlockSpec(memory_space=pl.ANY)],
-        out_specs=pl.BlockSpec(memory_space=pltpu.VMEM),
-        out_shape=jax.ShapeDtypeStruct(displacement.shape, jnp.float32),
+        out_specs=[vmem, vmem],
+        out_shape=[
+            jax.ShapeDtypeStruct(displacement.shape, jnp.float32),
+            jax.ShapeDtypeStruct((2, 3, col_count, row_count), jnp.float32),
+        ],
         scratch_shapes=[
             pltpu.VMEM((3, ply_count, 3 * col_count, row_count), jnp.float32),
             pltpu.VMEM((2, 3, col_count, row_count), jnp.float32),
@@ -249,6 +260,12 @@
         ],
         compiler_params=pltpu.CompilerParams(collective_id=0, has_side_effects=True),
     )(angle_index, bond_table, interface_stiffness, displacement)
+    return pl.pallas_call(
+        add_edges,
+        in_specs=[vmem, vmem],
+        out_specs=vmem,
+        out_shape=jax.ShapeDtypeStruct(displacement.shape, jnp.float32),
+    )(force, edges)
 
 
 def solution(mesh):

time: 37.6 us -> 37.7 us (level)
  Pallas kernels: 35.5 us -> 37.5 us
  local copies, waits for them, and re-layouts: 1.93 us -> 0 us
    pallas_call x0 -> x1, Pallas kernels: none -> 1.97 us  [local(): pl.pallas_call(add_edges, in_specs=[vmem, vmem], out_specs=vmem, out_shap...]
    unnamed x1 -> x0, local copies, waits for them, and re-layouts: 1.93 us -> none
where the time goes in v5:
time: 37.7 us; the launch traced here: 37.5 us
  Pallas kernels  37.5 us (99%)
    pallas_call x1, Pallas kernels, local(): pl.pallas_call(kernel, in_specs=[smem, smem, smem, pl.BlockSpec(memory_sp...  35.5 us
    pallas_call x1, Pallas kernels, local(): pl.pallas_call(add_edges, in_specs=[vmem, vmem], out_specs=vmem, out_shap...  1.97 us

profile of v5, /device:TPU:33, one launch (start us, length us, event | category | flops | bytes accessed | tf_op | source)
XLA Modules:
  0.0 37.5 jit_solution(16896099637296675674)
XLA Ops:
  0.0 35.5 %shard_map.46 = (f32[3,6,8,1024]{3,2,1,0:T(8,128)}, f32[2,3,8,1024]{3,2,1,0:T(8,128)}) custom-call(s32[6]{0:T(128)} %angle_ref.1, f32[4,14]{1,0:T(4,128)} %table_ref.1, f32[23]{0:T(128)} %spring_ref.1, f32[3,6,8,1024]{3,2,1,0:T(8,128)} %u_hbm.1), custom_call_target="tpu_custom_call" | custom-call | tf_op jit(solution)/shard_map/pallas_call | solution.py:243
  35.5 2.0 %shard_map.47 = f32[3,6,8,1024]{3,2,1,0:T(8,128)} custom-call(f32[3,6,8,1024]{3,2,1,0:T(8,128)} %get-tuple-element.7.force_ref, f32[2,3,8,1024]{3,2,1,0:T(8,128)} %get-tuple-element.8.edge_ref), custom_call_target="tpu_custom_call" | custom-call | tf_op jit(solution)/shard_map/pallas_call | solution.py:263

commit v6 on v4

--- a/solution.py
+++ b/solution.py
@@ -56,8 +56,8 @@
     shifts = sorted({a for a, _, _, _ in bonds})
     lanes = sorted({b for _, b, _, _ in bonds})
 
-    def kernel(angle_ref, table_ref, spring_ref, u_hbm, o_ref, ext, ply_halo, wq_ref, dmask_ref,
-               fmask_ref, sems, send_t, recv_t):
+    def kernel(angle_ref, table_ref, spring_ref, u_hbm, o_ref, ext, ply_halo, wq_ref, fmask_ref,
+               hmask_ref, wm_ref, sx_ref, sy_ref, sz_ref, pa_ref, pb_ref, sems, send_t, recv_t):
         t = lax.axis_index("tile")
         nt = lax.axis_size("tile")
         q = lax.axis_index("ply")
@@ -95,53 +95,54 @@
         for cond, cp in zip(has[2:], ply_copies):
             pl.when(cond)(cp.start)
 
-        def bond_masks(n, start, out_ref):
-            r = lax.broadcasted_iota(jnp.int32, (n, rows), 0) + (x0 + start)
-            c = lax.broadcasted_iota(jnp.int32, (n, rows), 1)
-            own_x = (r >= 0) & (r < x_total)
-            total = jnp.zeros((n, rows), jnp.float32)
+        sub = lax.broadcasted_iota(jnp.int32, (cols, rows), 0)
+        lane = lax.broadcasted_iota(jnp.int32, (cols, rows), 1)
+        core_x = sub + x0
+        edge_x = jnp.where(sub < 3, x0 - 3 + sub, x0 + cols - 3 + sub)
+        edge_ok = sub < 6
+
+        def bond_masks(xg, ok0, out_ref):
+            own_x = ok0 & (xg >= 0) & (xg < x_total)
+            total = jnp.zeros((cols, rows), jnp.float32)
             for i, (a, b, length, column) in enumerate(bonds):
-                ok = own_x & (r + a >= 0) & (r + a < x_total) & (c + b >= 0) & (c + b < rows)
+                ok = own_x & (xg + a >= 0) & (xg + a < x_total) & (lane + b >= 0) & (lane + b < rows)
                 m = jnp.where(ok, 1.0, 0.0)
                 out_ref[i] = m
                 total = total + m * length
             return total
 
-        mass = bond_masks(wide, -3, dmask_ref)
-        bond_masks(cols, 0, fmask_ref)
-        wq_ref[0] = jnp.where(mass > 0, 1.0 / jnp.where(mass > 0, mass, 1.0), 0.0)
-
-        @pl.when(t == 0)
-        def _():
-            ext[:, :, 0:cols, :] = jnp.zeros((3, plies, cols, rows), jnp.float32)
-
-        @pl.when(t == nt - 1)
-        def _():
-            ext[:, :, 2 * cols:3 * cols, :] = jnp.zeros((3, plies, cols, rows), jnp.float32)
-
-        @pl.when(q == 0)
-        def _():
-            ply_halo[0] = jnp.zeros((3, cols, rows), jnp.float32)
-
-        @pl.when(q == nq - 1)
-        def _():
-            ply_halo[1] = jnp.zeros((3, cols, rows), jnp.float32)
-
-        own.wait()
-
-        def masks(n, start):
-            r = lax.broadcasted_iota(jnp.int32, (n, rows), 0) + (x0 + start)
-            c = lax.broadcasted_iota(jnp.int32, (n, rows), 1)
-            own = (r >= 0) & (r < x_total)
-            xm = {a: own & (r + a >= 0) & (r + a < x_total) for a in shifts}
-            ym = {b: (c + b >= 0) & (c + b < rows) for b in lanes}
-            return xm, ym
-
-        base = cols - 3
-
+        mass_c = bond_masks(core_x, sub >= 0, fmask_ref)
+        mass_e = bond_masks(edge_x, edge_ok, hmask_ref)
+        w_c = 1.0 / jnp.where(mass_c > 0, mass_c, 1.0)
+        w_e = jnp.where(mass_e > 0, 1.0 / jnp.where(mass_e > 0, mass_e, 1.0), 0.0)
+        wq_ref[0, 0:3, :] = w_e[0:3]
+        wq_ref[0, 3:3 + cols, :] = w_c
+        wq_ref[0, 3 + cols:6 + cols, :] = w_e[3:6]
         groups = {}
         for i, (a, b, length, column) in enumerate(bonds):
             groups.setdefault(a, []).append((i, b, length, column))
+        for a, members in groups.items():
+            w_slab = wq_ref[0, 3 + a:3 + a + cols, :]
+            for i, b, length, column in members:
+                wm_ref[i] = fmask_ref[i] * (w_c + shift_lanes(w_slab, b))
+
+        @pl.when(t == 0)
+        def _():
+            ext[:, :, 0:cols, :] = jnp.zeros((3, plies, cols, rows), jnp.float32)
+
+        @pl.when(t == nt - 1)
+        def _():
+            ext[:, :, 2 * cols:3 * cols, :] = jnp.zeros((3, plies, cols, rows), jnp.float32)
+
+        @pl.when(q == 0)
+        def _():
+            ply_halo[0] = jnp.zeros((3, cols, rows), jnp.float32)
+
+        @pl.when(q == nq - 1)
+        def _():
+            ply_halo[1] = jnp.zeros((3, cols, rows), jnp.float32)
+
+        own.wait()
 
         def ply_body(p, carry):
             for d in range(2):
@@ -151,51 +152,61 @@
             pl.when(has[0])(tile_copy(1, p).wait_recv)
             gp = q * plies + p
             kind = angle_ref[p]
-            w = wq_ref[0]
-            ud = [ext[k, p, base:base + wide, :] for k in range(3)]
-            ud_y = {b: ud[1] - b for b in lanes}
-            dil = jnp.zeros((wide, rows), jnp.float32)
+            low = lax.broadcasted_iota(jnp.int32, (cols, rows), 0) < 3
+
+            def edge_rows(k, a):
+                return jnp.where(low, ext[k, p, cols - 3 + a:2 * cols - 3 + a, :],
+                                 ext[k, p, 2 * cols - 3 + a:3 * cols - 3 + a, :])
+
+            uc = [ext[k, p, cols:2 * cols, :] for k in range(3)]
+            ue = [edge_rows(k, 0) for k in range(3)]
+            uc_y = {b: uc[1] - b for b in lanes}
+            ue_y = {b: ue[1] - b for b in lanes}
+            dil_c = jnp.zeros((cols, rows), jnp.float32)
+            dil_e = jnp.zeros((cols, rows), jnp.float32)
             for a, members in groups.items():
-                slab = [ext[k, p, base + a:base + a + wide, :] for k in range(3)]
-                ud_x = ud[0] - a
+                cs = [ext[k, p, cols + a:2 * cols + a, :] for k in range(3)]
+                es = [edge_rows(k, a) for k in range(3)]
+                uc_x = uc[0] - a
+                ue_x = ue[0] - a
                 for i, b, length, column in members:
-                    sx = shift_lanes(slab[0], b) - ud_x
-                    sy = shift_lanes(slab[1], b) - ud_y[b]
-                    sz = shift_lanes(slab[2], b) - ud[2]
+                    sx = shift_lanes(cs[0], b) - uc_x
+                    sy = shift_lanes(cs[1], b) - uc_y[b]
+                    sz = shift_lanes(cs[2], b) - uc[2]
                     s2 = sx * sx + sy * sy + sz * sz
-                    span = s2 * lax.rsqrt(s2)
-                    dil = dil + (span - length) * dmask_ref[i]
-            theta = 3.0 * dil * w
-            wq_ref[1] = theta * w
-
-            uc = [ext[k, p, cols:2 * cols, :] for k in range(3)]
-            uc_y = {b: uc[1] - b for b in lanes}
-            wi = wq_ref[0, 3:3 + cols, :]
-            qi = wq_ref[1, 3:3 + cols, :]
+                    inv = lax.rsqrt(s2)
+                    e = s2 * inv - length
+                    m = fmask_ref[i]
+                    dil_c = dil_c + e * m
+                    sx_ref[i] = sx
+                    sy_ref[i] = sy
+                    sz_ref[i] = sz
+                    pa_ref[i] = (inv * e) * wm_ref[i]
+                    pb_ref[i] = inv * m
+                    hx = shift_lanes(es[0], b) - ue_x
+                    hy = shift_lanes(es[1], b) - ue_y[b]
+                    hz = shift_lanes(es[2], b) - ue[2]
+                    h2 = hx * hx + hy * hy + hz * hz
+                    dil_e = dil_e + (h2 * lax.rsqrt(h2) - length) * hmask_ref[i]
+            q_c = (3.0 * dil_c * w_c) * w_c
+            q_e = (3.0 * dil_e * w_e) * w_e
+            wq_ref[1, 0:3, :] = q_e[0:3]
+            wq_ref[1, 3:3 + cols, :] = q_c
+            wq_ref[1, 3 + cols:6 + cols, :] = q_e[3:6]
+
             fx = jnp.zeros((cols, rows), jnp.float32)
             fy = jnp.zeros((cols, rows), jnp.float32)
             fz = jnp.zeros((cols, rows), jnp.float32)
             for a, members in groups.items():
-                slab = [ext[k, p, cols + a:2 * cols + a, :] for k in range(3)]
-                w_slab = wq_ref[0, 3 + a:3 + a + cols, :]
                 q_slab = wq_ref[1, 3 + a:3 + a + cols, :]
-                uc_x = uc[0] - a
                 for i, b, length, column in members:
-                    sx = shift_lanes(slab[0], b) - uc_x
-                    sy = shift_lanes(slab[1], b) - uc_y[b]
-                    sz = shift_lanes(slab[2], b) - uc[2]
-                    s2 = sx * sx + sy * sy + sz * sz
-                    inv = lax.rsqrt(s2)
-                    span = s2 * inv
                     shear = table_ref[kind, column]
                     alpha = shear * (15.0 / length)
                     beta = 3.0 * bulk_modulus - 5.0 * shear
-                    tb = alpha * (span - length) * (wi + shift_lanes(w_slab, b)) + beta * (
-                        qi + shift_lanes(q_slab, b))
-                    f = (tb * inv) * fmask_ref[i]
-                    fx = fx + f * sx
-                    fy = fy + f * sy
-                    fz = fz + f * sz
+                    f = alpha * pa_ref[i] + beta * (pb_ref[i] * (q_c + shift_lanes(q_slab, b)))
+                    fx = fx + f * sx_ref[i]
+                    fy = fy + f * sy_ref[i]
+                    fz = fz + f * sz_ref[i]
             above = jnp.where(gp < nsprings, spring_ref[jnp.minimum(gp, nsprings - 1)], 0.0)
             below = jnp.where(gp > 0, spring_ref[jnp.maximum(gp - 1, 0)], 0.0)
             hi_p = jnp.minimum(p + 1, plies - 1)
@@ -241,7 +252,13 @@
             pltpu.VMEM((3, ply_count, 3 * col_count, row_count), jnp.float32),
             pltpu.VMEM((2, 3, col_count, row_count), jnp.float32),
             pltpu.VMEM((2, col_count + 6, row_count), jnp.float32),
-            pltpu.VMEM((nbond, col_count + 6, row_count), jnp.float32),
+            pltpu.VMEM((nbond, col_count, row_count), jnp.float32),
+            pltpu.VMEM((nbond, col_count, row_count), jnp.float32),
+            pltpu.VMEM((nbond, col_count, row_count), jnp.float32),
+            pltpu.VMEM((nbond, col_count, row_count), jnp.float32),
+            pltpu.VMEM((nbond, col_count, row_count), jnp.float32),
+            pltpu.VMEM((nbond, col_count, row_count), jnp.float32),
+            pltpu.VMEM((nbond, col_count, row_count), jnp.float32),
             pltpu.VMEM((nbond, col_count, row_count), jnp.float32),
             pltpu.SemaphoreType.DMA((5,)),
             pltpu.SemaphoreType.DMA((2, ply_count)),

time: 37.6 us -> 34.6 us (0.920)
  the two profiles are of different devices: /device:TPU:33 before, /device:TPU:224 now
where the time goes in v6:
time: 34.6 us; the launch traced here: 34.4 us
  Pallas kernels  32.5 us (94%)
  local copies, waits for them, and re-layouts  1.93 us (6%)
    pallas_call x1, Pallas kernels, local(): pl.pallas_call(kernel, in_specs=[smem, smem, smem, pl.BlockSpec(memory_sp...  32.5 us
    unnamed x1, local copies, waits for them, and re-layouts  1.93 us

profile of v6, /device:TPU:224, one launch (start us, length us, event | category | flops | bytes accessed | tf_op | source)
XLA Modules:
  0.0 34.4 jit_solution(11882233366606711209)
XLA Ops:
  0.0 32.5 %shard_map.46 = f32[3,6,8,1024]{3,2,1,0:T(8,128)} custom-call(s32[6]{0:T(128)} %angle_ref.1, f32[4,14]{1,0:T(4,128)} %table_ref.1, f32[23]{0:T(128)} %spring_ref.1, f32[3,6,8,1024]{3,2,1,0:T(8,128)} %u_hbm.1), custom_call_target="tpu_custom_call" | custom-call | tf_op jit(solution)/shard_map/pallas_call | solution.py:246
  32.5 1.9 %copy.6 = f32[3,6,8,1024]{3,2,1,0:T(8,128)} copy(f32[3,6,8,1024]{3,2,1,0:T(8,128)} %shard_map.46) | data formatting | bytes 1179648

commit v7 on v6

--- a/solution.py
+++ b/solution.py
@@ -75,9 +75,12 @@
         count = sum(c.astype(jnp.int32) for c in has)
         pl.semaphore_wait(barrier, count)
         def tile_copy(d, p):
-            rows_at = slice(2 * cols, 3 * cols) if d == 0 else slice(0, cols)
+            if d == 0:
+                src, dst = slice(0, 6), slice(2 * cols, 2 * cols + 6)
+            else:
+                src, dst = slice(cols - 6, cols), slice(cols - 6, cols)
             return pltpu.make_async_remote_copy(
-                u_hbm.at[:, p], ext.at[:, p, rows_at, :], send_t.at[d, p], recv_t.at[d, p],
+                u_hbm.at[:, p, src, :], ext.at[:, p, dst, :], send_t.at[d, p], recv_t.at[d, p],
                 device_id=peers[d], device_id_type=MESH)
 
         ply_copies = (

time: 34.6 us -> 32 us (0.925)
  the two profiles are of different devices: /device:TPU:224 before, /device:TPU:33 now
where the time goes in v7:
time: 32 us; the launch traced here: 31.8 us
  Pallas kernels  29.8 us (93%)
  local copies, waits for them, and re-layouts  1.93 us (6%)
    pallas_call x1, Pallas kernels, local(): pl.pallas_call(kernel, in_specs=[smem, smem, smem, pl.BlockSpec(memory_sp...  29.8 us
    unnamed x1, local copies, waits for them, and re-layouts  1.93 us

profile of v7, /device:TPU:33, one launch (start us, length us, event | category | flops | bytes accessed | tf_op | source)
XLA Modules:
  0.0 31.8 jit_solution(6969205132105795183)
XLA Ops:
  0.0 29.8 %shard_map.46 = f32[3,6,8,1024]{3,2,1,0:T(8,128)} custom-call(s32[6]{0:T(128)} %angle_ref.1, f32[4,14]{1,0:T(4,128)} %table_ref.1, f32[23]{0:T(128)} %spring_ref.1, f32[3,6,8,1024]{3,2,1,0:T(8,128)} %u_hbm.1), custom_call_target="tpu_custom_call" | custom-call | tf_op jit(solution)/shard_map/pallas_call | solution.py:249
  29.9 1.9 %copy.6 = f32[3,6,8,1024]{3,2,1,0:T(8,128)} copy(f32[3,6,8,1024]{3,2,1,0:T(8,128)} %shard_map.46) | data formatting | bytes 1179648

commit v8 on v7

--- a/solution.py
+++ b/solution.py
@@ -91,7 +91,7 @@
                 u_hbm.at[:, plies - 1], ply_halo.at[0], sems.at[2], sems.at[4],
                 device_id=peers[3], device_id_type=MESH),
         )
-        ahead = min(2, plies)
+        ahead = plies
         for p in range(ahead):
             for d in range(2):
                 pl.when(has[d])(tile_copy(d, p).start)

time: 32 us -> 32 us (level)
  no operation moved by 1% of the time
where the time goes in v8:
time: 32 us; the launch traced here: 31.8 us
  Pallas kernels  29.8 us (93%)
  local copies, waits for them, and re-layouts  1.93 us (6%)
    pallas_call x1, Pallas kernels, local(): pl.pallas_call(kernel, in_specs=[smem, smem, smem, pl.BlockSpec(memory_sp...  29.8 us
    unnamed x1, local copies, waits for them, and re-layouts  1.93 us

profile of v8, /device:TPU:33, one launch (start us, length us, event | category | flops | bytes accessed | tf_op | source)
XLA Modules:
  0.0 31.8 jit_solution(1298730265575195647)
XLA Ops:
  0.0 29.8 %shard_map.46 = f32[3,6,8,1024]{3,2,1,0:T(8,128)} custom-call(s32[6]{0:T(128)} %angle_ref.1, f32[4,14]{1,0:T(4,128)} %table_ref.1, f32[23]{0:T(128)} %spring_ref.1, f32[3,6,8,1024]{3,2,1,0:T(8,128)} %u_hbm.1), custom_call_target="tpu_custom_call" | custom-call | tf_op jit(solution)/shard_map/pallas_call | solution.py:249
  29.9 1.9 %copy.6 = f32[3,6,8,1024]{3,2,1,0:T(8,128)} copy(f32[3,6,8,1024]{3,2,1,0:T(8,128)} %shard_map.46) | data formatting | bytes 1179648

commit v9 on v7

--- a/solution.py
+++ b/solution.py
@@ -56,7 +56,7 @@
     shifts = sorted({a for a, _, _, _ in bonds})
     lanes = sorted({b for _, b, _, _ in bonds})
 
-    def kernel(angle_ref, table_ref, spring_ref, u_hbm, o_ref, ext, ply_halo, wq_ref, fmask_ref,
+    def kernel(angle_ref, table_ref, spring_ref, u_hbm, o_ref, ext, wq_ref, fmask_ref,
                hmask_ref, wm_ref, sx_ref, sy_ref, sz_ref, pa_ref, pb_ref, sems, send_t, recv_t):
         t = lax.axis_index("tile")
         nt = lax.axis_size("tile")
@@ -65,8 +65,8 @@
         x0 = t * cols
         own = pltpu.make_async_copy(u_hbm, ext.at[:, :, cols:2 * cols, :], sems.at[0])
         own.start()
-        has = ((t > 0), (t < nt - 1), (q > 0), (q < nq - 1))
-        peers = ({"tile": t - 1}, {"tile": t + 1}, {"ply": q - 1}, {"ply": q + 1})
+        has = ((t > 0), (t < nt - 1))
+        peers = ({"tile": t - 1}, {"tile": t + 1})
         barrier = pltpu.get_barrier_semaphore()
         for cond, dev in zip(has, peers):
             @pl.when(cond)
@@ -83,20 +83,10 @@
                 u_hbm.at[:, p, src, :], ext.at[:, p, dst, :], send_t.at[d, p], recv_t.at[d, p],
                 device_id=peers[d], device_id_type=MESH)
 
-        ply_copies = (
-            pltpu.make_async_remote_copy(
-                u_hbm.at[:, 0], ply_halo.at[1], sems.at[1], sems.at[3],
-                device_id=peers[2], device_id_type=MESH),
-            pltpu.make_async_remote_copy(
-                u_hbm.at[:, plies - 1], ply_halo.at[0], sems.at[2], sems.at[4],
-                device_id=peers[3], device_id_type=MESH),
-        )
         ahead = min(2, plies)
         for p in range(ahead):
             for d in range(2):
                 pl.when(has[d])(tile_copy(d, p).start)
-        for cond, cp in zip(has[2:], ply_copies):
-            pl.when(cond)(cp.start)
 
         sub = lax.broadcasted_iota(jnp.int32, (cols, rows), 0)
         lane = lax.broadcasted_iota(jnp.int32, (cols, rows), 1)
@@ -136,14 +126,6 @@
         @pl.when(t == nt - 1)
         def _():
             ext[:, :, 2 * cols:3 * cols, :] = jnp.zeros((3, plies, cols, rows), jnp.float32)
-
-        @pl.when(q == 0)
-        def _():
-            ply_halo[0] = jnp.zeros((3, cols, rows), jnp.float32)
-
-        @pl.when(q == nq - 1)
-        def _():
-            ply_halo[1] = jnp.zeros((3, cols, rows), jnp.float32)
 
         own.wait()
 
@@ -221,21 +203,9 @@
             return carry
 
         lax.fori_loop(0, plies, ply_body, 0)
-        pl.when(has[3])(ply_copies[0].wait_recv)
-        pl.when(has[2])(ply_copies[1].wait_recv)
-        g0 = q * plies
-        below = jnp.where(g0 > 0, spring_ref[jnp.maximum(g0 - 1, 0)], 0.0)
-        gl = q * plies + plies - 1
-        above = jnp.where(gl < nsprings, spring_ref[jnp.minimum(gl, nsprings - 1)], 0.0)
-        for k in range(3):
-            o_ref[k, 0] = o_ref[k, 0] + below * (ply_halo[0, k] - ext[k, 0, cols:2 * cols, :])
-            o_ref[k, plies - 1] = o_ref[k, plies - 1] + above * (
-                ply_halo[1, k] - ext[k, plies - 1, cols:2 * cols, :])
         for p in range(plies):
             for d in range(2):
                 pl.when(has[d])(tile_copy(d, p).wait_send)
-        for cond, cp in zip(has[2:], ply_copies):
-            pl.when(cond)(cp.wait_send)
 
     return kernel
 
@@ -246,14 +216,13 @@
     kernel = make_kernel(ply_count, col_count, row_count, x_total, interface_stiffness.shape[0])
     nbond = len(bond_list())
     smem = pl.BlockSpec(memory_space=pltpu.SMEM)
-    return pl.pallas_call(
+    force = pl.pallas_call(
         kernel,
         in_specs=[smem, smem, smem, pl.BlockSpec(memory_space=pl.ANY)],
         out_specs=pl.BlockSpec(memory_space=pltpu.VMEM),
         out_shape=jax.ShapeDtypeStruct(displacement.shape, jnp.float32),
         scratch_shapes=[
             pltpu.VMEM((3, ply_count, 3 * col_count, row_count), jnp.float32),
-            pltpu.VMEM((2, 3, col_count, row_count), jnp.float32),
             pltpu.VMEM((2, col_count + 6, row_count), jnp.float32),
             pltpu.VMEM((nbond, col_count, row_count), jnp.float32),
             pltpu.VMEM((nbond, col_count, row_count), jnp.float32),
@@ -269,6 +238,20 @@
         ],
         compiler_params=pltpu.CompilerParams(collective_id=0, has_side_effects=True),
     )(angle_index, bond_table, interface_stiffness, displacement)
+    peers = lax.axis_size("ply")
+    up = [(i, i + 1) for i in range(peers - 1)]
+    down = [(i + 1, i) for i in range(peers - 1)]
+    lo = lax.ppermute(displacement[:, ply_count - 1], "ply", up)
+    hi = lax.ppermute(displacement[:, 0], "ply", down)
+    zero_end = jnp.zeros((1,), jnp.float32)
+    coupling = jnp.concatenate([zero_end, interface_stiffness, zero_end])
+    local_coupling = lax.dynamic_slice_in_dim(
+        coupling, lax.axis_index("ply") * ply_count, ply_count + 1
+    )
+    first = force[:, 0] + local_coupling[0] * (lo - displacement[:, 0])
+    last = force[:, ply_count - 1] + local_coupling[ply_count] * (
+        hi - displacement[:, ply_count - 1])
+    return force.at[:, 0].set(first).at[:, ply_count - 1].set(last)
 
 
 def solution(mesh):

time: 32 us -> 53.1 us (1.66)
  starting transfers between devices: 0 us -> 10.4 us
  waiting for transfers between devices: 0 us -> 7.96 us
  other arithmetic: 0 us -> 3.86 us
  Pallas kernels: 29.8 us -> 28.2 us
    ppermute x0 -> x2, starting transfers between devices: none -> 10.4 us  [the longest x1 8.47 us: local(): lo = lax.ppermute(displacement[:, ply_count - 1], 'ply', up)]
    ppermute x0 -> x2, waiting for transfers between devices: none -> 7.96 us  [the longest x1 7.96 us: local(): hi = lax.ppermute(displacement[:, 0], 'ply', down)]
    scatter x0 -> x1, other arithmetic: none -> 2.23 us  [local(): return force.at[:, 0].set(first).at[:, ply_count - 1].set(last)]
    pallas_call x1, Pallas kernels: 29.8 us -> 28.2 us  [local(): pl.pallas_call(kernel, in_specs=[smem, smem, smem, pl.BlockSpec(memory_sp...]
    squeeze x0 -> x1, other arithmetic: none -> 1.56 us  [local(): first = force[:, 0] + local_coupling[0] * (lo - displacement[:, 0])]
    unnamed x1 -> x8, local copies, waits for them, and re-layouts: 1.93 us -> 0.63 us
    squeeze x0 -> x1, local copies, waits for them, and re-layouts: none -> 0.9 us  [local(): lo = lax.ppermute(displacement[:, ply_count - 1], 'ply', up)]
    slice x0 -> x3, local copies, waits for them, and re-layouts: none -> 0.65 us  [the longest x1 0.65 us: local(): local_coupling[ply_count] * (hi - displacement[:, ply_count - 1])]
  transfers between devices with their start and end apart: 0 -> 2, of which waited for: 0 -> 1; matrix products, arithmetic and copies ran while one was open for 0% -> 2% of each run, Pallas kernels for 0% -> 53%
where the time goes in v9:
time: 53.1 us; the launch traced here: 52.8 us
  Pallas kernels  28.2 us (53%)
  starting transfers between devices  10.4 us (20%)
  waiting for transfers between devices  7.96 us (15%)
  other arithmetic  3.86 us (7%)
  local copies, waits for them, and re-layouts  2.26 us (4%)
    pallas_call x1, Pallas kernels, local(): pl.pallas_call(kernel, in_specs=[smem, smem, smem, pl.BlockSpec(memory_sp...  28.2 us
    ppermute x1, starting transfers between devices, local(): lo = lax.ppermute(displacement[:, ply_count - 1], 'ply', up)  8.47 us
    ppermute x1, waiting for transfers between devices, local(): hi = lax.ppermute(displacement[:, 0], 'ply', down)  7.96 us
    scatter x1, other arithmetic, local(): return force.at[:, 0].set(first).at[:, ply_count - 1].set(last)  2.23 us
    ppermute x1, starting transfers between devices, local(): hi = lax.ppermute(displacement[:, 0], 'ply', down)  1.92 us
    squeeze x1, other arithmetic, local(): first = force[:, 0] + local_coupling[0] * (lo - displacement[:, 0])  1.56 us
  transfers between devices with their start and end apart: 2, of which 1 were waited for; matrix products, arithmetic and copies ran while one was open for 2% of the time, Pallas kernels for 53%

profile of v9, /device:TPU:33, one launch (start us, length us, event | category | flops | bytes accessed | tf_op | source)
XLA Modules:
  0.0 52.8 jit_solution(15366289056407030172)
XLA Ops:
  0.0 0.9 %slice_bitcast_fusion.1 = f32[3,8,1024]{2,1,0:T(8,128)S(1)} fusion(f32[3,6,8,1024]{3,2,1,0:T(8,128)} %u_hbm.1), kind=kLoop, calls=%fused_computation.6 | loop fusion | bytes 196608 | tf_op jit(solution)/shard_map/squeeze | solution.py:244
  0.9 8.5 %collective-permute-start = (f32[3,8,1024]{2,1,0:T(8,128)S(1)}, f32[3,8,1024]{2,1,0:T(8,128)S(1)}, u32[]{:S(2)}, u32[]{:S(2)}) collective-permute-start(f32[3,8,1024]{2,1,0:T(8,128)S(1)} %slice_bitcast_fusion.1), channel_id=1, source_target_pairs={{0,64},{64,128},{128,192},{1,65},{65,129},{129,193},{2,66},{66,130... | collective-permute-start | bytes 294920 | tf_op jit(solution)/shard_map/ppermute | solution.py:244
  9.4 28.2 %shard_map.46 = f32[3,6,8,1024]{3,2,1,0:T(8,128)} custom-call(s32[6]{0:T(128)} %angle_ref.1, f32[4,14]{1,0:T(4,128)} %table_ref.1, f32[23]{0:T(128)} %spring_ref.1, f32[3,6,8,1024]{3,2,1,0:T(8,128)} %u_hbm.1), custom_call_target="tpu_custom_call" | custom-call | tf_op jit(solution)/shard_map/pallas_call | solution.py:219
  37.6 0.0 copy-start.3
  37.6 0.0 slice-start
  37.6 0.0 copy-start.2
  37.6 0.0 copy-start
  37.7 0.6 %copy-done.3 = f32[23]{0:T(128)S(1)} copy-done((f32[23]{0:T(128)S(1)}, f32[23]{0:T(128)}, u32[]{:S(2)}) %copy-start.3) | copy-done | bytes 116
  38.3 0.1 pad_maximum_fusion
  38.3 0.1 dynamic_slice.3
  38.4 0.7 %fusion.2 = (f32[1]{0:T(128)}, f32[1]{0:T(128)}) fusion(f32[7]{0:T(128)S(1)} %dynamic_slice.3), kind=kLoop, calls=%fused_computation.8 | loop fusion | bytes 16 | tf_op jit(solution)/shard_map/slice | solution.py:252
  39.1 0.0 collective-permute-done
  39.1 0.0 slice-done
  39.1 0.0 copy-done.2
  39.1 1.6 %slice_bitcast_fusion = (f32[3,8,1024]{2,1,0:T(8,128)S(1)}, f32[3,6,8,1024]{3,2,1,0:T(8,128)S(1)}) fusion(f32[3,6,8,1024]{3,2,1,0:T(8,128)} %u_hbm.1, f32[3,6,8,1024]{3,2,1,0:T(8,128)S(1)} %copy-done.2, f32[3,8,1024]{2,1,0:T(8,128)S(1)} %collective-permute-done, f32[]{:T(128)} %bitcast.1, f32[3,1,8,1024]{3,2,1,0:T(8,128)S(1)} %slice-done), kind=kLoop, calls=%fused_computation.5 | loop fusion | flops 73728 | bytes 491524 | tf_op jit(solution)/shard_map/squeeze | solution.py:251
  40.6 0.0 copy-start.1
  40.7 1.9 %collective-permute-start.1 = (f32[3,8,1024]{2,1,0:T(8,128)S(1)}, f32[3,8,1024]{2,1,0:T(8,128)S(1)}, u32[]{:S(2)}, u32[]{:S(2)}) collective-permute-start(f32[3,8,1024]{2,1,0:T(8,128)S(1)} %get-tuple-element.29), channel_id=1, source_target_pairs={{64,0},{128,64},{192,128},{65,1},{129,65},{193,129},{66,2},{130,66... | collective-permute-start | bytes 294920 | tf_op jit(solution)/shard_map/ppermute | solution.py:245
  42.6 8.0 %collective-permute-done.1 = f32[3,8,1024]{2,1,0:T(8,128)S(1)} collective-permute-done((f32[3,8,1024]{2,1,0:T(8,128)S(1)}, f32[3,8,1024]{2,1,0:T(8,128)S(1)}, u32[]{:S(2)}, u32[]{:S(2)}) %collective-permute-start.1) | collective-permute-done | bytes 98336 | tf_op jit(solution)/shard_map/ppermute | solution.py:245
  50.5 0.0 copy-done.1
  50.5 0.0 copy-done
  50.5 2.2 %bitcast_dynamic-update-slice_fusion = f32[3,6,8,1024]{3,2,1,0:T(8,128)} fusion(f32[3,6,8,1024]{3,2,1,0:T(8,128)} %copy-done.1, f32[3,8,1024]{2,1,0:T(8,128)S(1)} %collective-permute-done.1, f32[3,6,8,1024]{3,2,1,0:T(8,128)S(1)} %copy-done, f32[]{:T(128)} %bitcast.7, f32[3,6,8,1024]{3,2,1,0:T(8,128)} %u_hbm.1), kind=kLoop, calls=%fused_computation.3 | loop fusion | flops 73728 | bytes 393728 | tf_op jit(solution)/shard_map/scatter | solution.py:254
Async XLA Ops:
  0.9 38.2 %collective-permute-start = (f32[3,8,1024]{2,1,0:T(8,128)S(1)}, f32[3,8,1024]{2,1,0:T(8,128)S(1)}, u32[]{:S(2)}, u32[]{:S(2)}) collective-permute-start(f32[3,8,1024]{2,1,0:T(8,128)S(1)} %slice_bitcast_fusion.1), channel_id=1, source_target_pairs={{0,64},{64,128},{128,192},{1,65},{65,129},{129,193},{2,66},{66,130... | collective-permute-start | bytes 294920 | tf_op jit(solution)/shard_map/ppermute | solution.py:244
  37.6 0.7 %copy-start.3 = (f32[23]{0:T(128)S(1)}, f32[23]{0:T(128)}, u32[]{:S(2)}) copy-start(f32[23]{0:T(128)} %spring_ref.1) | copy-start | bytes 280
  37.6 1.5 %slice-start = ((f32[3,6,8,1024]{3,2,1,0:T(8,128)}), f32[3,1,8,1024]{3,2,1,0:T(8,128)S(1)}, s32[]{:S(2)}) async-start(f32[3,6,8,1024]{3,2,1,0:T(8,128)} %shard_map.46), calls=%async_computation | async-start | bytes 196608 | tf_op jit(solution)/shard_map/slice | solution.py:251
  37.6 1.4 %copy-start.2 = (f32[3,6,8,1024]{3,2,1,0:T(8,128)S(1)}, f32[3,6,8,1024]{3,2,1,0:T(8,128)}, u32[]{:S(2)}) copy-start(f32[3,6,8,1024]{3,2,1,0:T(8,128)} %shard_map.46) | copy-start | bytes 1769476
  37.6 12.9 %copy-start = (f32[3,6,8,1024]{3,2,1,0:T(8,128)S(1)}, f32[3,6,8,1024]{3,2,1,0:T(8,128)}, u32[]{:S(2)}) copy-start(f32[3,6,8,1024]{3,2,1,0:T(8,128)} %shard_map.46) | copy-start | bytes 1769476
  40.6 9.9 %copy-start.1 = (f32[3,6,8,1024]{3,2,1,0:T(8,128)}, f32[3,6,8,1024]{3,2,1,0:T(8,128)S(1)}, u32[]{:S(2)}) copy-start(f32[3,6,8,1024]{3,2,1,0:T(8,128)S(1)} %get-tuple-element.30) | copy-start | bytes 1769476
  40.7 9.9 %collective-permute-start.1 = (f32[3,8,1024]{2,1,0:T(8,128)S(1)}, f32[3,8,1024]{2,1,0:T(8,128)S(1)}, u32[]{:S(2)}, u32[]{:S(2)}) collective-permute-start(f32[3,8,1024]{2,1,0:T(8,128)S(1)} %get-tuple-element.29), channel_id=1, source_target_pairs={{64,0},{128,64},{192,128},{65,1},{129,65},{193,129},{66,2},{130,66... | collective-permute-start | bytes 294920 | tf_op jit(solution)/shard_map/ppermute | solution.py:245

commit v10 on v7

--- a/solution.py
+++ b/solution.py
@@ -57,7 +57,8 @@
     lanes = sorted({b for _, b, _, _ in bonds})
 
     def kernel(angle_ref, table_ref, spring_ref, u_hbm, o_ref, ext, ply_halo, wq_ref, fmask_ref,
-               hmask_ref, wm_ref, sx_ref, sy_ref, sz_ref, pa_ref, pb_ref, sems, send_t, recv_t):
+               hmask_ref, wm_ref, sx_ref, sy_ref, sz_ref, pa_ref, pb_ref, qx_ref, sems, send_t,
+               recv_t, send_q, recv_q):
         t = lax.axis_index("tile")
         nt = lax.axis_size("tile")
         q = lax.axis_index("ply")
@@ -76,11 +77,20 @@
         pl.semaphore_wait(barrier, count)
         def tile_copy(d, p):
             if d == 0:
-                src, dst = slice(0, 6), slice(2 * cols, 2 * cols + 6)
+                src, dst = slice(0, 3), slice(2 * cols, 2 * cols + 3)
             else:
-                src, dst = slice(cols - 6, cols), slice(cols - 6, cols)
+                src, dst = slice(cols - 3, cols), slice(cols - 3, cols)
             return pltpu.make_async_remote_copy(
                 u_hbm.at[:, p, src, :], ext.at[:, p, dst, :], send_t.at[d, p], recv_t.at[d, p],
+                device_id=peers[d], device_id_type=MESH)
+
+        def q_copy(d, p):
+            if d == 0:
+                src, dst = slice(cols, cols + 3), slice(2 * cols, 2 * cols + 3)
+            else:
+                src, dst = slice(2 * cols - 3, 2 * cols), slice(cols - 3, cols)
+            return pltpu.make_async_remote_copy(
+                qx_ref.at[p, src, :], qx_ref.at[p, dst, :], send_q.at[d, p], recv_q.at[d, p],
                 device_id=peers[d], device_id_type=MESH)
 
         ply_copies = (
@@ -132,10 +142,12 @@
         @pl.when(t == 0)
         def _():
             ext[:, :, 0:cols, :] = jnp.zeros((3, plies, cols, rows), jnp.float32)
+            qx_ref[:, 0:cols, :] = jnp.zeros((plies, cols, rows), jnp.float32)
 
         @pl.when(t == nt - 1)
         def _():
             ext[:, :, 2 * cols:3 * cols, :] = jnp.zeros((3, plies, cols, rows), jnp.float32)
+            qx_ref[:, 2 * cols:3 * cols, :] = jnp.zeros((plies, cols, rows), jnp.float32)
 
         @pl.when(q == 0)
         def _():
@@ -147,31 +159,19 @@
 
         own.wait()
 
-        def ply_body(p, carry):
+        def dil_phase(p):
+            slot = p % 2
             for d in range(2):
                 pl.when(has[d] & (p + ahead < plies))(
                     lambda d=d: tile_copy(d, jnp.minimum(p + ahead, plies - 1)).start())
             pl.when(has[1])(tile_copy(0, p).wait_recv)
             pl.when(has[0])(tile_copy(1, p).wait_recv)
-            gp = q * plies + p
-            kind = angle_ref[p]
-            low = lax.broadcasted_iota(jnp.int32, (cols, rows), 0) < 3
-
-            def edge_rows(k, a):
-                return jnp.where(low, ext[k, p, cols - 3 + a:2 * cols - 3 + a, :],
-                                 ext[k, p, 2 * cols - 3 + a:3 * cols - 3 + a, :])
-
             uc = [ext[k, p, cols:2 * cols, :] for k in range(3)]
-            ue = [edge_rows(k, 0) for k in range(3)]
             uc_y = {b: uc[1] - b for b in lanes}
-            ue_y = {b: ue[1] - b for b in lanes}
             dil_c = jnp.zeros((cols, rows), jnp.float32)
-            dil_e = jnp.zeros((cols, rows), jnp.float32)
             for a, members in groups.items():
                 cs = [ext[k, p, cols + a:2 * cols + a, :] for k in range(3)]
-                es = [edge_rows(k, a) for k in range(3)]
                 uc_x = uc[0] - a
-                ue_x = ue[0] - a
                 for i, b, length, column in members:
                     sx = shift_lanes(cs[0], b) - uc_x
                     sy = shift_lanes(cs[1], b) - uc_y[b]
@@ -181,35 +181,37 @@
                     e = s2 * inv - length
                     m = fmask_ref[i]
                     dil_c = dil_c + e * m
-                    sx_ref[i] = sx
-                    sy_ref[i] = sy
-                    sz_ref[i] = sz
-                    pa_ref[i] = (inv * e) * wm_ref[i]
-                    pb_ref[i] = inv * m
-                    hx = shift_lanes(es[0], b) - ue_x
-                    hy = shift_lanes(es[1], b) - ue_y[b]
-                    hz = shift_lanes(es[2], b) - ue[2]
-                    h2 = hx * hx + hy * hy + hz * hz
-                    dil_e = dil_e + (h2 * lax.rsqrt(h2) - length) * hmask_ref[i]
-            q_c = (3.0 * dil_c * w_c) * w_c
-            q_e = (3.0 * dil_e * w_e) * w_e
-            wq_ref[1, 0:3, :] = q_e[0:3]
-            wq_ref[1, 3:3 + cols, :] = q_c
-            wq_ref[1, 3 + cols:6 + cols, :] = q_e[3:6]
-
+                    sx_ref[slot, i] = sx
+                    sy_ref[slot, i] = sy
+                    sz_ref[slot, i] = sz
+                    pa_ref[slot, i] = (inv * e) * wm_ref[i]
+                    pb_ref[slot, i] = inv * m
+            qx_ref[p, cols:2 * cols, :] = (3.0 * dil_c * w_c) * w_c
+            for d in range(2):
+                pl.when(has[d])(q_copy(d, p).start)
+
+        def force_phase(p):
+            slot = p % 2
+            gp = q * plies + p
+            kind = angle_ref[p]
+            pl.when(has[1])(q_copy(0, p).wait_recv)
+            pl.when(has[0])(q_copy(1, p).wait_recv)
+            uc = [ext[k, p, cols:2 * cols, :] for k in range(3)]
+            q_c = qx_ref[p, cols:2 * cols, :]
             fx = jnp.zeros((cols, rows), jnp.float32)
             fy = jnp.zeros((cols, rows), jnp.float32)
             fz = jnp.zeros((cols, rows), jnp.float32)
             for a, members in groups.items():
-                q_slab = wq_ref[1, 3 + a:3 + a + cols, :]
+                q_slab = qx_ref[p, cols + a:2 * cols + a, :]
                 for i, b, length, column in members:
                     shear = table_ref[kind, column]
                     alpha = shear * (15.0 / length)
                     beta = 3.0 * bulk_modulus - 5.0 * shear
-                    f = alpha * pa_ref[i] + beta * (pb_ref[i] * (q_c + shift_lanes(q_slab, b)))
-                    fx = fx + f * sx_ref[i]
-                    fy = fy + f * sy_ref[i]
-                    fz = fz + f * sz_ref[i]
+                    f = alpha * pa_ref[slot, i] + beta * (
+                        pb_ref[slot, i] * (q_c + shift_lanes(q_slab, b)))
+                    fx = fx + f * sx_ref[slot, i]
+                    fy = fy + f * sy_ref[slot, i]
+                    fz = fz + f * sz_ref[slot, i]
             above = jnp.where(gp < nsprings, spring_ref[jnp.minimum(gp, nsprings - 1)], 0.0)
             below = jnp.where(gp > 0, spring_ref[jnp.maximum(gp - 1, 0)], 0.0)
             hi_p = jnp.minimum(p + 1, plies - 1)
@@ -218,6 +220,12 @@
                 hi = jnp.where(p == plies - 1, uc[k], ext[k, hi_p, cols:2 * cols, :])
                 lo = jnp.where(p == 0, uc[k], ext[k, lo_p, cols:2 * cols, :])
                 o_ref[k, p] = fk + (above * (hi - uc[k]) + below * (lo - uc[k]))
+
+        dil_phase(0)
+
+        def ply_body(p, carry):
+            pl.when(p + 1 < plies)(lambda: dil_phase(jnp.minimum(p + 1, plies - 1)))
+            force_phase(p)
             return carry
 
         lax.fori_loop(0, plies, ply_body, 0)
@@ -234,6 +242,7 @@
         for p in range(plies):
             for d in range(2):
                 pl.when(has[d])(tile_copy(d, p).wait_send)
+                pl.when(has[d])(q_copy(d, p).wait_send)
         for cond, cp in zip(has[2:], ply_copies):
             pl.when(cond)(cp.wait_send)
 
@@ -258,12 +267,15 @@
             pltpu.VMEM((nbond, col_count, row_count), jnp.float32),
             pltpu.VMEM((nbond, col_count, row_count), jnp.float32),
             pltpu.VMEM((nbond, col_count, row_count), jnp.float32),
-            pltpu.VMEM((nbond, col_count, row_count), jnp.float32),
-            pltpu.VMEM((nbond, col_count, row_count), jnp.float32),
-            pltpu.VMEM((nbond, col_count, row_count), jnp.float32),
-            pltpu.VMEM((nbond, col_count, row_count), jnp.float32),
-            pltpu.VMEM((nbond, col_count, row_count), jnp.float32),
+            pltpu.VMEM((2, nbond, col_count, row_count), jnp.float32),
+            pltpu.VMEM((2, nbond, col_count, row_count), jnp.float32),
+            pltpu.VMEM((2, nbond, col_count, row_count), jnp.float32),
+            pltpu.VMEM((2, nbond, col_count, row_count), jnp.float32),
+            pltpu.VMEM((2, nbond, col_count, row_count), jnp.float32),
+            pltpu.VMEM((ply_count, 3 * col_count, row_count), jnp.float32),
             pltpu.SemaphoreType.DMA((5,)),
+            pltpu.SemaphoreType.DMA((2, ply_count)),
+            pltpu.SemaphoreType.DMA((2, ply_count)),
             pltpu.SemaphoreType.DMA((2, ply_count)),
             pltpu.SemaphoreType.DMA((2, ply_count)),
         ],

time: 32 us -> 36.4 us (1.14)
  the two profiles are of different devices: /device:TPU:33 before, /device:TPU:192 now
where the time goes in v10:
time: 36.4 us; the launch traced here: 36.2 us
  Pallas kernels  34.3 us (94%)
  local copies, waits for them, and re-layouts  1.93 us (5%)
    pallas_call x1, Pallas kernels, local(): pl.pallas_call(kernel, in_specs=[smem, smem, smem, pl.BlockSpec(memory_sp...  34.3 us
    unnamed x1, local copies, waits for them, and re-layouts  1.93 us

profile of v10, /device:TPU:192, one launch (start us, length us, event | category | flops | bytes accessed | tf_op | source)
XLA Modules:
  0.0 36.2 jit_solution(8900522329201871928)
XLA Ops:
  0.0 34.3 %shard_map.46 = f32[3,6,8,1024]{3,2,1,0:T(8,128)} custom-call(s32[6]{0:T(128)} %angle_ref.1, f32[4,14]{1,0:T(4,128)} %table_ref.1, f32[23]{0:T(128)} %spring_ref.1, f32[3,6,8,1024]{3,2,1,0:T(8,128)} %u_hbm.1), custom_call_target="tpu_custom_call" | custom-call | tf_op jit(solution)/shard_map/pallas_call | solution.py:258
  34.3 1.9 %copy.6 = f32[3,6,8,1024]{3,2,1,0:T(8,128)} copy(f32[3,6,8,1024]{3,2,1,0:T(8,128)} %shard_map.46) | data formatting | bytes 1179648

commit v11 on v10

--- a/solution.py
+++ b/solution.py
@@ -57,7 +57,7 @@
     lanes = sorted({b for _, b, _, _ in bonds})
 
     def kernel(angle_ref, table_ref, spring_ref, u_hbm, o_ref, ext, ply_halo, wq_ref, fmask_ref,
-               hmask_ref, wm_ref, sx_ref, sy_ref, sz_ref, pa_ref, pb_ref, qx_ref, sems, send_t,
+               hmask_ref, wm_ref, qx_ref, sems, send_t,
                recv_t, send_q, recv_q):
         t = lax.axis_index("tile")
         nt = lax.axis_size("tile")
@@ -178,14 +178,7 @@
                     sz = shift_lanes(cs[2], b) - uc[2]
                     s2 = sx * sx + sy * sy + sz * sz
                     inv = lax.rsqrt(s2)
-                    e = s2 * inv - length
-                    m = fmask_ref[i]
-                    dil_c = dil_c + e * m
-                    sx_ref[slot, i] = sx
-                    sy_ref[slot, i] = sy
-                    sz_ref[slot, i] = sz
-                    pa_ref[slot, i] = (inv * e) * wm_ref[i]
-                    pb_ref[slot, i] = inv * m
+                    dil_c = dil_c + (s2 * inv - length) * fmask_ref[i]
             qx_ref[p, cols:2 * cols, :] = (3.0 * dil_c * w_c) * w_c
             for d in range(2):
                 pl.when(has[d])(q_copy(d, p).start)
@@ -197,21 +190,31 @@
             pl.when(has[1])(q_copy(0, p).wait_recv)
             pl.when(has[0])(q_copy(1, p).wait_recv)
             uc = [ext[k, p, cols:2 * cols, :] for k in range(3)]
+            uc_y = {b: uc[1] - b for b in lanes}
             q_c = qx_ref[p, cols:2 * cols, :]
             fx = jnp.zeros((cols, rows), jnp.float32)
             fy = jnp.zeros((cols, rows), jnp.float32)
             fz = jnp.zeros((cols, rows), jnp.float32)
             for a, members in groups.items():
+                cs = [ext[k, p, cols + a:2 * cols + a, :] for k in range(3)]
+                uc_x = uc[0] - a
                 q_slab = qx_ref[p, cols + a:2 * cols + a, :]
                 for i, b, length, column in members:
+                    sx = shift_lanes(cs[0], b) - uc_x
+                    sy = shift_lanes(cs[1], b) - uc_y[b]
+                    sz = shift_lanes(cs[2], b) - uc[2]
+                    s2 = sx * sx + sy * sy + sz * sz
+                    inv = lax.rsqrt(s2)
+                    e = s2 * inv - length
                     shear = table_ref[kind, column]
                     alpha = shear * (15.0 / length)
                     beta = 3.0 * bulk_modulus - 5.0 * shear
-                    f = alpha * pa_ref[slot, i] + beta * (
-                        pb_ref[slot, i] * (q_c + shift_lanes(q_slab, b)))
-                    fx = fx + f * sx_ref[slot, i]
-                    fy = fy + f * sy_ref[slot, i]
-                    fz = fz + f * sz_ref[slot, i]
+                    tb = alpha * e * wm_ref[i] + beta * (
+                        fmask_ref[i] * (q_c + shift_lanes(q_slab, b)))
+                    f = tb * inv
+                    fx = fx + f * sx
+                    fy = fy + f * sy
+                    fz = fz + f * sz
             above = jnp.where(gp < nsprings, spring_ref[jnp.minimum(gp, nsprings - 1)], 0.0)
             below = jnp.where(gp > 0, spring_ref[jnp.maximum(gp - 1, 0)], 0.0)
             hi_p = jnp.minimum(p + 1, plies - 1)
@@ -221,14 +224,16 @@
                 lo = jnp.where(p == 0, uc[k], ext[k, lo_p, cols:2 * cols, :])
                 o_ref[k, p] = fk + (above * (hi - uc[k]) + below * (lo - uc[k]))
 
-        dil_phase(0)
-
-        def ply_body(p, carry):
-            pl.when(p + 1 < plies)(lambda: dil_phase(jnp.minimum(p + 1, plies - 1)))
+        def dil_body(p, carry):
+            dil_phase(p)
+            return carry
+
+        def force_body(p, carry):
             force_phase(p)
             return carry
 
-        lax.fori_loop(0, plies, ply_body, 0)
+        lax.fori_loop(0, plies, dil_body, 0)
+        lax.fori_loop(0, plies, force_body, 0)
         pl.when(has[3])(ply_copies[0].wait_recv)
         pl.when(has[2])(ply_copies[1].wait_recv)
         g0 = q * plies
@@ -267,11 +272,6 @@
             pltpu.VMEM((nbond, col_count, row_count), jnp.float32),
             pltpu.VMEM((nbond, col_count, row_count), jnp.float32),
             pltpu.VMEM((nbond, col_count, row_count), jnp.float32),
-            pltpu.VMEM((2, nbond, col_count, row_count), jnp.float32),
-            pltpu.VMEM((2, nbond, col_count, row_count), jnp.float32),
-            pltpu.VMEM((2, nbond, col_count, row_count), jnp.float32),
-            pltpu.VMEM((2, nbond, col_count, row_count), jnp.float32),
-            pltpu.VMEM((2, nbond, col_count, row_count), jnp.float32),
             pltpu.VMEM((ply_count, 3 * col_count, row_count), jnp.float32),
             pltpu.SemaphoreType.DMA((5,)),
             pltpu.SemaphoreType.DMA((2, ply_count)),

time: 36.4 us -> 34.7 us (0.953)
  the two profiles are of different devices: /device:TPU:192 before, /device:TPU:224 now
where the time goes in v11:
time: 34.7 us; the launch traced here: 34.5 us
  Pallas kernels  32.6 us (94%)
  local copies, waits for them, and re-layouts  1.93 us (6%)
    pallas_call x1, Pallas kernels, local(): pl.pallas_call(kernel, in_specs=[smem, smem, smem, pl.BlockSpec(memory_sp...  32.6 us
    unnamed x1, local copies, waits for them, and re-layouts  1.93 us

profile of v11, /device:TPU:224, one launch (start us, length us, event | category | flops | bytes accessed | tf_op | source)
XLA Modules:
  0.0 34.5 jit_solution(18299173643241895604)
XLA Ops:
  0.0 32.6 %shard_map.46 = f32[3,6,8,1024]{3,2,1,0:T(8,128)} custom-call(s32[6]{0:T(128)} %angle_ref.1, f32[4,14]{1,0:T(4,128)} %table_ref.1, f32[23]{0:T(128)} %spring_ref.1, f32[3,6,8,1024]{3,2,1,0:T(8,128)} %u_hbm.1), custom_call_target="tpu_custom_call" | custom-call | tf_op jit(solution)/shard_map/pallas_call | solution.py:263
  32.6 1.9 %copy.6 = f32[3,6,8,1024]{3,2,1,0:T(8,128)} copy(f32[3,6,8,1024]{3,2,1,0:T(8,128)} %shard_map.46) | data formatting | bytes 1179648

commit v12 on v7

--- a/solution.py
+++ b/solution.py
@@ -95,8 +95,6 @@
         for p in range(ahead):
             for d in range(2):
                 pl.when(has[d])(tile_copy(d, p).start)
-        for cond, cp in zip(has[2:], ply_copies):
-            pl.when(cond)(cp.start)
 
         sub = lax.broadcasted_iota(jnp.int32, (cols, rows), 0)
         lane = lax.broadcasted_iota(jnp.int32, (cols, rows), 1)
@@ -153,6 +151,8 @@
                     lambda d=d: tile_copy(d, jnp.minimum(p + ahead, plies - 1)).start())
             pl.when(has[1])(tile_copy(0, p).wait_recv)
             pl.when(has[0])(tile_copy(1, p).wait_recv)
+            for cond, cp in zip(has[2:], ply_copies):
+                pl.when(cond & (p == min(2, plies - 1)))(cp.start)
             gp = q * plies + p
             kind = angle_ref[p]
             low = lax.broadcasted_iota(jnp.int32, (cols, rows), 0) < 3

time: 32 us -> 32.7 us (1.022)
  the two profiles are of different devices: /device:TPU:33 before, /device:TPU:160 now
where the time goes in v12:
time: 32.7 us; the launch traced here: 32.5 us
  Pallas kernels  30.5 us (93%)
  local copies, waits for them, and re-layouts  1.93 us (6%)
    pallas_call x1, Pallas kernels, local(): pl.pallas_call(kernel, in_specs=[smem, smem, smem, pl.BlockSpec(memory_sp...  30.5 us
    unnamed x1, local copies, waits for them, and re-layouts  1.93 us

profile of v12, /device:TPU:160, one launch (start us, length us, event | category | flops | bytes accessed | tf_op | source)
XLA Modules:
  0.0 32.5 jit_solution(2628838189816061491)
XLA Ops:
  0.0 30.5 %shard_map.46 = f32[3,6,8,1024]{3,2,1,0:T(8,128)} custom-call(s32[6]{0:T(128)} %angle_ref.1, f32[4,14]{1,0:T(4,128)} %table_ref.1, f32[23]{0:T(128)} %spring_ref.1, f32[3,6,8,1024]{3,2,1,0:T(8,128)} %u_hbm.1), custom_call_target="tpu_custom_call" | custom-call | tf_op jit(solution)/shard_map/pallas_call | solution.py:249
  30.5 1.9 %copy.6 = f32[3,6,8,1024]{3,2,1,0:T(8,128)} copy(f32[3,6,8,1024]{3,2,1,0:T(8,128)} %shard_map.46) | data formatting | bytes 1179648

commit v13 on v8

--- a/solution.py
+++ b/solution.py
@@ -91,7 +91,7 @@
                 u_hbm.at[:, plies - 1], ply_halo.at[0], sems.at[2], sems.at[4],
                 device_id=peers[3], device_id_type=MESH),
         )
-        ahead = plies
+        ahead = 1
         for p in range(ahead):
             for d in range(2):
                 pl.when(has[d])(tile_copy(d, p).start)

time: 32 us -> 37.5 us (1.17)
  Pallas kernels: 29.8 us -> 35.3 us
    pallas_call x1, Pallas kernels: 29.8 us -> 35.3 us  [local(): pl.pallas_call(kernel, in_specs=[smem, smem, smem, pl.BlockSpec(memory_sp...]
where the time goes in v13:
time: 37.5 us; the launch traced here: 37.3 us
  Pallas kernels  35.3 us (94%)
  local copies, waits for them, and re-layouts  1.93 us (5%)
    pallas_call x1, Pallas kernels, local(): pl.pallas_call(kernel, in_specs=[smem, smem, smem, pl.BlockSpec(memory_sp...  35.3 us
    unnamed x1, local copies, waits for them, and re-layouts  1.93 us

profile of v13, /device:TPU:33, one launch (start us, length us, event | category | flops | bytes accessed | tf_op | source)
XLA Modules:
  0.0 37.3 jit_solution(10876043813714782113)
XLA Ops:
  0.0 35.3 %shard_map.46 = f32[3,6,8,1024]{3,2,1,0:T(8,128)} custom-call(s32[6]{0:T(128)} %angle_ref.1, f32[4,14]{1,0:T(4,128)} %table_ref.1, f32[23]{0:T(128)} %spring_ref.1, f32[3,6,8,1024]{3,2,1,0:T(8,128)} %u_hbm.1), custom_call_target="tpu_custom_call" | custom-call | tf_op jit(solution)/shard_map/pallas_call | solution.py:249
  35.3 1.9 %copy.6 = f32[3,6,8,1024]{3,2,1,0:T(8,128)} copy(f32[3,6,8,1024]{3,2,1,0:T(8,128)} %shard_map.46) | data formatting | bytes 1179648

commit v14 on v7

--- a/solution.py
+++ b/solution.py
@@ -184,7 +184,7 @@
                     sx_ref[i] = sx
                     sy_ref[i] = sy
                     sz_ref[i] = sz
-                    pa_ref[i] = (inv * e) * wm_ref[i]
+                    pa_ref[i] = e * wm_ref[i]
                     pb_ref[i] = inv * m
                     hx = shift_lanes(es[0], b) - ue_x
                     hy = shift_lanes(es[1], b) - ue_y[b]
@@ -206,7 +206,7 @@
                     shear = table_ref[kind, column]
                     alpha = shear * (15.0 / length)
                     beta = 3.0 * bulk_modulus - 5.0 * shear
-                    f = alpha * pa_ref[i] + beta * (pb_ref[i] * (q_c + shift_lanes(q_slab, b)))
+                    f = pb_ref[i] * (alpha * pa_ref[i] + beta * (q_c + shift_lanes(q_slab, b)))
                     fx = fx + f * sx_ref[i]
                     fy = fy + f * sy_ref[i]
                     fz = fz + f * sz_ref[i]

time: 32 us -> 32 us (level)
  no operation moved by 1% of the time
where the time goes in v14:
time: 32 us; the launch traced here: 31.8 us
  Pallas kernels  29.9 us (93%)
  local copies, waits for them, and re-layouts  1.93 us (6%)
    pallas_call x1, Pallas kernels, local(): pl.pallas_call(kernel, in_specs=[smem, smem, smem, pl.BlockSpec(memory_sp...  29.9 us
    unnamed x1, local copies, waits for them, and re-layouts  1.93 us

profile of v14, /device:TPU:33, one launch (start us, length us, event | category | flops | bytes accessed | tf_op | source)
XLA Modules:
  0.0 31.8 jit_solution(17831828238047887210)
XLA Ops:
  0.0 29.9 %shard_map.46 = f32[3,6,8,1024]{3,2,1,0:T(8,128)} custom-call(s32[6]{0:T(128)} %angle_ref.1, f32[4,14]{1,0:T(4,128)} %table_ref.1, f32[23]{0:T(128)} %spring_ref.1, f32[3,6,8,1024]{3,2,1,0:T(8,128)} %u_hbm.1), custom_call_target="tpu_custom_call" | custom-call | tf_op jit(solution)/shard_map/pallas_call | solution.py:249
  29.9 1.9 %copy.6 = f32[3,6,8,1024]{3,2,1,0:T(8,128)} copy(f32[3,6,8,1024]{3,2,1,0:T(8,128)} %shard_map.46) | data formatting | bytes 1179648

commit v15 on v14

--- a/solution.py
+++ b/solution.py
@@ -91,7 +91,7 @@
                 u_hbm.at[:, plies - 1], ply_halo.at[0], sems.at[2], sems.at[4],
                 device_id=peers[3], device_id_type=MESH),
         )
-        ahead = min(2, plies)
+        ahead = min(3, plies)
         for p in range(ahead):
             for d in range(2):
                 pl.when(has[d])(tile_copy(d, p).start)

time: 32 us -> 32 us (level)
  no operation moved by 1% of the time
where the time goes in v15:
time: 32 us; the launch traced here: 31.8 us
  Pallas kernels  29.9 us (93%)
  local copies, waits for them, and re-layouts  1.93 us (6%)
    pallas_call x1, Pallas kernels, local(): pl.pallas_call(kernel, in_specs=[smem, smem, smem, pl.BlockSpec(memory_sp...  29.9 us
    unnamed x1, local copies, waits for them, and re-layouts  1.93 us

profile of v15, /device:TPU:33, one launch (start us, length us, event | category | flops | bytes accessed | tf_op | source)
XLA Modules:
  0.0 31.8 jit_solution(4778339991129338909)
XLA Ops:
  0.0 29.9 %shard_map.46 = f32[3,6,8,1024]{3,2,1,0:T(8,128)} custom-call(s32[6]{0:T(128)} %angle_ref.1, f32[4,14]{1,0:T(4,128)} %table_ref.1, f32[23]{0:T(128)} %spring_ref.1, f32[3,6,8,1024]{3,2,1,0:T(8,128)} %u_hbm.1), custom_call_target="tpu_custom_call" | custom-call | tf_op jit(solution)/shard_map/pallas_call | solution.py:249
  29.9 1.9 %copy.6 = f32[3,6,8,1024]{3,2,1,0:T(8,128)} copy(f32[3,6,8,1024]{3,2,1,0:T(8,128)} %shard_map.46) | data formatting | bytes 1179648

commit v16 on v7

--- a/solution.py
+++ b/solution.py
@@ -146,6 +146,15 @@
             ply_halo[1] = jnp.zeros((3, cols, rows), jnp.float32)
 
         own.wait()
+        for p in range(plies):
+            gp = q * plies + p
+            above = jnp.where(gp < nsprings, spring_ref[jnp.minimum(gp, nsprings - 1)], 0.0)
+            below = jnp.where(gp > 0, spring_ref[jnp.maximum(gp - 1, 0)], 0.0)
+            for k in range(3):
+                u_p = ext[k, p, cols:2 * cols, :]
+                hi = ext[k, p + 1, cols:2 * cols, :] if p + 1 < plies else u_p
+                lo = ext[k, p - 1, cols:2 * cols, :] if p > 0 else u_p
+                o_ref[k, p] = above * (hi - u_p) + below * (lo - u_p)
 
         def ply_body(p, carry):
             for d in range(2):
@@ -210,14 +219,8 @@
                     fx = fx + f * sx_ref[i]
                     fy = fy + f * sy_ref[i]
                     fz = fz + f * sz_ref[i]
-            above = jnp.where(gp < nsprings, spring_ref[jnp.minimum(gp, nsprings - 1)], 0.0)
-            below = jnp.where(gp > 0, spring_ref[jnp.maximum(gp - 1, 0)], 0.0)
-            hi_p = jnp.minimum(p + 1, plies - 1)
-            lo_p = jnp.maximum(p - 1, 0)
             for k, fk in enumerate((fx, fy, fz)):
-                hi = jnp.where(p == plies - 1, uc[k], ext[k, hi_p, cols:2 * cols, :])
-                lo = jnp.where(p == 0, uc[k], ext[k, lo_p, cols:2 * cols, :])
-                o_ref[k, p] = fk + (above * (hi - uc[k]) + below * (lo - uc[k]))
+                o_ref[k, p] = fk + o_ref[k, p]
             return carry
 
         lax.fori_loop(0, plies, ply_body, 0)

time: 32 us -> 31.8 us (level)
  no operation moved by 1% of the time
where the time goes in v16:
time: 31.8 us; the launch traced here: 31.7 us
  Pallas kernels  29.7 us (93%)
  local copies, waits for them, and re-layouts  1.93 us (6%)
    pallas_call x1, Pallas kernels, local(): pl.pallas_call(kernel, in_specs=[smem, smem, smem, pl.BlockSpec(memory_sp...  29.7 us
    unnamed x1, local copies, waits for them, and re-layouts  1.93 us

profile of v16, /device:TPU:33, one launch (start us, length us, event | category | flops | bytes accessed | tf_op | source)
XLA Modules:
  0.0 31.7 jit_solution(7588765754775906136)
XLA Ops:
  0.0 29.7 %shard_map.46 = f32[3,6,8,1024]{3,2,1,0:T(8,128)} custom-call(s32[6]{0:T(128)} %angle_ref.1, f32[4,14]{1,0:T(4,128)} %table_ref.1, f32[23]{0:T(128)} %spring_ref.1, f32[3,6,8,1024]{3,2,1,0:T(8,128)} %u_hbm.1), custom_call_target="tpu_custom_call" | custom-call | tf_op jit(solution)/shard_map/pallas_call | solution.py:252
  29.7 1.9 %copy.6 = f32[3,6,8,1024]{3,2,1,0:T(8,128)} copy(f32[3,6,8,1024]{3,2,1,0:T(8,128)} %shard_map.46) | data formatting | bytes 1179648

commit v17 on v7

--- a/solution.py
+++ b/solution.py
@@ -76,11 +76,11 @@
         pl.semaphore_wait(barrier, count)
         def tile_copy(d, p):
             if d == 0:
-                src, dst = slice(0, 6), slice(2 * cols, 2 * cols + 6)
+                src, dst = slice(cols, cols + 6), slice(2 * cols, 2 * cols + 6)
             else:
-                src, dst = slice(cols - 6, cols), slice(cols - 6, cols)
+                src, dst = slice(2 * cols - 6, 2 * cols), slice(cols - 6, cols)
             return pltpu.make_async_remote_copy(
-                u_hbm.at[:, p, src, :], ext.at[:, p, dst, :], send_t.at[d, p], recv_t.at[d, p],
+                ext.at[:, p, src, :], ext.at[:, p, dst, :], send_t.at[d, p], recv_t.at[d, p],
                 device_id=peers[d], device_id_type=MESH)
 
         ply_copies = (
@@ -92,6 +92,7 @@
                 device_id=peers[3], device_id_type=MESH),
         )
         ahead = min(2, plies)
+        own.wait()
         for p in range(ahead):
             for d in range(2):
                 pl.when(has[d])(tile_copy(d, p).start)
@@ -145,7 +146,6 @@
         def _():
             ply_halo[1] = jnp.zeros((3, cols, rows), jnp.float32)
 
-        own.wait()
 
         def ply_body(p, carry):
             for d in range(2):

time: 32 us -> 31.7 us (level)
  no operation moved by 1% of the time
where the time goes in v17:
time: 31.7 us; the launch traced here: 31.5 us
  Pallas kernels  29.6 us (93%)
  local copies, waits for them, and re-layouts  1.93 us (6%)
    pallas_call x1, Pallas kernels, local(): pl.pallas_call(kernel, in_specs=[smem, smem, smem, pl.BlockSpec(memory_sp...  29.6 us
    unnamed x1, local copies, waits for them, and re-layouts  1.93 us

profile of v17, /device:TPU:33, one launch (start us, length us, event | category | flops | bytes accessed | tf_op | source)
XLA Modules:
  0.0 31.5 jit_solution(12472327660120541034)
XLA Ops:
  0.0 29.6 %shard_map.46 = f32[3,6,8,1024]{3,2,1,0:T(8,128)} custom-call(s32[6]{0:T(128)} %angle_ref.1, f32[4,14]{1,0:T(4,128)} %table_ref.1, f32[23]{0:T(128)} %spring_ref.1, f32[3,6,8,1024]{3,2,1,0:T(8,128)} %u_hbm.1), custom_call_target="tpu_custom_call" | custom-call | tf_op jit(solution)/shard_map/pallas_call | solution.py:249
  29.6 1.9 %copy.6 = f32[3,6,8,1024]{3,2,1,0:T(8,128)} copy(f32[3,6,8,1024]{3,2,1,0:T(8,128)} %shard_map.46) | data formatting | bytes 1179648

commit v18 on v16

--- a/solution.py
+++ b/solution.py
@@ -76,11 +76,11 @@
         pl.semaphore_wait(barrier, count)
         def tile_copy(d, p):
             if d == 0:
-                src, dst = slice(0, 6), slice(2 * cols, 2 * cols + 6)
+                src, dst = slice(cols, cols + 6), slice(2 * cols, 2 * cols + 6)
             else:
-                src, dst = slice(cols - 6, cols), slice(cols - 6, cols)
+                src, dst = slice(2 * cols - 6, 2 * cols), slice(cols - 6, cols)
             return pltpu.make_async_remote_copy(
-                u_hbm.at[:, p, src, :], ext.at[:, p, dst, :], send_t.at[d, p], recv_t.at[d, p],
+                ext.at[:, p, src, :], ext.at[:, p, dst, :], send_t.at[d, p], recv_t.at[d, p],
                 device_id=peers[d], device_id_type=MESH)
 
         ply_copies = (
@@ -92,6 +92,7 @@
                 device_id=peers[3], device_id_type=MESH),
         )
         ahead = min(2, plies)
+        own.wait()
         for p in range(ahead):
             for d in range(2):
                 pl.when(has[d])(tile_copy(d, p).start)
@@ -145,7 +146,7 @@
         def _():
             ply_halo[1] = jnp.zeros((3, cols, rows), jnp.float32)
 
-        own.wait()
+
         for p in range(plies):
             gp = q * plies + p
             above = jnp.where(gp < nsprings, spring_ref[jnp.minimum(gp, nsprings - 1)], 0.0)
@@ -193,7 +194,7 @@
                     sx_ref[i] = sx
                     sy_ref[i] = sy
                     sz_ref[i] = sz
-                    pa_ref[i] = (inv * e) * wm_ref[i]
+                    pa_ref[i] = e * wm_ref[i]
                     pb_ref[i] = inv * m
                     hx = shift_lanes(es[0], b) - ue_x
                     hy = shift_lanes(es[1], b) - ue_y[b]
@@ -215,7 +216,7 @@
                     shear = table_ref[kind, column]
                     alpha = shear * (15.0 / length)
                     beta = 3.0 * bulk_modulus - 5.0 * shear
-                    f = alpha * pa_ref[i] + beta * (pb_ref[i] * (q_c + shift_lanes(q_slab, b)))
+                    f = pb_ref[i] * (alpha * pa_ref[i] + beta * (q_c + shift_lanes(q_slab, b)))
                     fx = fx + f * sx_ref[i]
                     fy = fy + f * sy_ref[i]
                     fz = fz + f * sz_ref[i]

time: 31.8 us -> 31.7 us (level)
  no operation moved by 1% of the time
where the time goes in v18:
time: 31.7 us; the launch traced here: 31.5 us
  Pallas kernels  29.5 us (93%)
  local copies, waits for them, and re-layouts  1.93 us (6%)
    pallas_call x1, Pallas kernels, local(): pl.pallas_call(kernel, in_specs=[smem, smem, smem, pl.BlockSpec(memory_sp...  29.5 us
    unnamed x1, local copies, waits for them, and re-layouts  1.93 us

profile of v18, /device:TPU:33, one launch (start us, length us, event | category | flops | bytes accessed | tf_op | source)
XLA Modules:
  0.0 31.5 jit_solution(8033336743036394162)
XLA Ops:
  0.0 29.5 %shard_map.46 = f32[3,6,8,1024]{3,2,1,0:T(8,128)} custom-call(s32[6]{0:T(128)} %angle_ref.1, f32[4,14]{1,0:T(4,128)} %table_ref.1, f32[23]{0:T(128)} %spring_ref.1, f32[3,6,8,1024]{3,2,1,0:T(8,128)} %u_hbm.1), custom_call_target="tpu_custom_call" | custom-call | tf_op jit(solution)/shard_map/pallas_call | solution.py:253
  29.5 1.9 %copy.6 = f32[3,6,8,1024]{3,2,1,0:T(8,128)} copy(f32[3,6,8,1024]{3,2,1,0:T(8,128)} %shard_map.46) | data formatting | bytes 1179648

commit v19 on v17

--- a/solution.py
+++ b/solution.py
@@ -85,10 +85,10 @@
 
         ply_copies = (
             pltpu.make_async_remote_copy(
-                u_hbm.at[:, 0], ply_halo.at[1], sems.at[1], sems.at[3],
+                ext.at[:, 0, cols:2 * cols, :], ply_halo.at[1], sems.at[1], sems.at[3],
                 device_id=peers[2], device_id_type=MESH),
             pltpu.make_async_remote_copy(
-                u_hbm.at[:, plies - 1], ply_halo.at[0], sems.at[2], sems.at[4],
+                ext.at[:, plies - 1, cols:2 * cols, :], ply_halo.at[0], sems.at[2], sems.at[4],
                 device_id=peers[3], device_id_type=MESH),
         )
         ahead = min(2, plies)

time: 31.7 us -> 31.7 us (level)
  no operation moved by 1% of the time
where the time goes in v19:
time: 31.7 us; the launch traced here: 31.5 us
  Pallas kernels  29.6 us (93%)
  local copies, waits for them, and re-layouts  1.93 us (6%)
    pallas_call x1, Pallas kernels, local(): pl.pallas_call(kernel, in_specs=[smem, smem, smem, pl.BlockSpec(memory_sp...  29.6 us
    unnamed x1, local copies, waits for them, and re-layouts  1.93 us

profile of v19, /device:TPU:33, one launch (start us, length us, event | category | flops | bytes accessed | tf_op | source)
XLA Modules:
  0.0 31.5 jit_solution(15219992523033838444)
XLA Ops:
  0.0 29.6 %shard_map.46 = f32[3,6,8,1024]{3,2,1,0:T(8,128)} custom-call(s32[6]{0:T(128)} %angle_ref.1, f32[4,14]{1,0:T(4,128)} %table_ref.1, f32[23]{0:T(128)} %spring_ref.1, f32[3,6,8,1024]{3,2,1,0:T(8,128)} %u_hbm.1), custom_call_target="tpu_custom_call" | custom-call | tf_op jit(solution)/shard_map/pallas_call | solution.py:249
  29.6 1.9 %copy.6 = f32[3,6,8,1024]{3,2,1,0:T(8,128)} copy(f32[3,6,8,1024]{3,2,1,0:T(8,128)} %shard_map.46) | data formatting | bytes 1179648
